TPU v7x, 32 devices: a whole 2x2x4 slice. The times are simulated.
32 devices in a mesh: group: 2 (over y), frame: 16 (over z, x, core).
Axes of the slice: x: 2, y: 2, z: 4, core: 2. Of those that a mesh axis runs over, the one named last changes fastest.
Arguments:
- queries: bfloat16 [8192, 1536], P(('group', 'frame')), parts along dimension 0, may hold values from -120 to 120, as said below
- key_rows: bfloat16 [8192, 1536], P(('group', 'frame')), parts along dimension 0, may hold values from -6 to 6, as said below
- value_rows: bfloat16 [8192, 1536], P(('group', 'frame')), parts along dimension 0, may hold values from -6 to 6
- out_grad: bfloat16 [8192, 1536], P(('group', 'frame')), parts along dimension 0, may hold values from -6 to 6
- block_mask: int32 [32, 4, 2], P(('group', 'frame')), parts along dimension 0, may hold values 0 or 1
- block_pick: int32 [32, 4], P(('group', 'frame')), parts along dimension 0, may hold values from 0 to 1
Outputs:
- attended: bfloat16 [8192, 1536], P(('group', 'frame')), parts along dimension 0
- query_grad: bfloat16 [8192, 1536], P(('group', 'frame')), parts along dimension 0
- key_grad: bfloat16 [8192, 1536], P(('group', 'frame')), parts along dimension 0
- value_grad: bfloat16 [8192, 1536], P(('group', 'frame')), parts along dimension 0
There are 2 independent parts, one for each index of `group`. A program takes and returns all parts, laid end to end along the dimension named above; each array names one. Nothing has to cross between parts.
Inputs may be any that keep to these rules, and one draw needn't show every extreme that they name: queries of order one; in some draws a few rows are strongly aligned with the keys of two consecutive rows. `key_rows`: keys of order one.
All inputs are finite; a program needn't handle non-finite values. No bound on the sum of `block_mask` on one device may be relied on, other than what follows from the above.
Results may differ from a plain program's by a relative error of at most 0.0054.
Values may be sent and summed in bfloat16 or wider, within the bound.
No kernel may reach another device: no remote copies, remote signals or barrier semaphores. Data moves between devices by JAX's collectives and lax.ppermute only.
A program may use at most 128 MiB of HBM per device.

v0:
```python
import functools

import jax
import jax.numpy as jnp
from jax import lax
from jax.experimental import pallas as pl
from jax.experimental.pallas import tpu as pltpu
from jax.sharding import PartitionSpec as P

HDIM = 128
BLK = 128
EDGE = 64
SCALE = HDIM ** (-0.5)
LOG2E = 1.4426950408889634
MASKED = -1e30
SPLIT = (6, 6)
PAIR = -1
BEYOND = -2

F32 = jnp.float32
BF16 = jnp.bfloat16
ANY = pl.BlockSpec(memory_space=pl.ANY)
NT = (((1,), (1,)), ((), ()))
TN = (((0,), (0,)), ((), ()))


def dot(lhs, rhs, dims=(((1,), (0,)), ((), ()))):
    return lax.dot_general(lhs, rhs, dims, preferred_element_type=F32)


def hbm(arrays):
    return [pltpu.with_memory_space_constraint(x, pltpu.HBM) for x in arrays]


def vmem(arrays):
    return [pltpu.with_memory_space_constraint(x, pltpu.VMEM) for x in arrays]


def cost(flops, moved, exps=0):
    return pl.CostEstimate(flops=flops, bytes_accessed=moved, transcendentals=exps)


def start_of(kind, pick_ref, tokens):
    odd = lax.axis_index("frame") % 2
    if kind == PAIR:
        return pl.multiple_of((1 - odd) * (tokens - EDGE), EDGE)
    if kind == BEYOND:
        return pl.multiple_of(odd * (tokens - EDGE), EDGE)
    return pl.multiple_of(pick_ref[0, kind] * BLK, BLK)


def pack_kernel(pieces, pick_ref, k_ref, v_ref, *rest):
    outs, sem = rest[:-1], rest[-1]
    copies = []
    for out, (parts, col, width) in zip(outs, pieces, strict=True):
        at = 0
        for kind, size in parts:
            start = start_of(kind, pick_ref, k_ref.shape[0])
            for side, src in enumerate((k_ref, v_ref)):
                copies.append(
                    pltpu.make_async_copy(
                        src.at[pl.ds(start, size), pl.ds(col, width)],
                        out.at[side, pl.ds(at, size)],
                        sem.at[len(copies)],
                    )
                )
            at += size
    for copy in copies:
        copy.start()
    for copy in copies:
        copy.wait()


def pack(picks, keys, values, pieces):
    sizes = [sum(size for _, size in parts) for parts, _, _ in pieces]
    return pl.pallas_call(
        functools.partial(pack_kernel, pieces),
        out_shape=[
            pltpu.VMEM((2, size, width), BF16)
            for size, (_, _, width) in zip(sizes, pieces, strict=True)
        ],
        in_specs=[pl.BlockSpec(memory_space=pltpu.SMEM), ANY, ANY],
        out_specs=[ANY] * len(pieces),
        scratch_shapes=[pltpu.SemaphoreType.DMA((2 * sum(len(parts) for parts, _, _ in pieces),))],
        compiler_params=pltpu.CompilerParams(vmem_limit_bytes=1 << 20),
        cost_estimate=cost(
            0, sum(8 * size * width for size, (_, _, width) in zip(sizes, pieces, strict=True))
        ),
    )(picks, *hbm((keys, values)))


def bias_columns(mask_ref, tokens, blocks, rows):
    frame, frames = lax.axis_index("frame"), lax.axis_size("frame")
    lane = lax.broadcasted_iota(jnp.int32, (1, HDIM), 1)
    pieces = [jnp.zeros((tokens, HDIM), BF16)]
    for parts in rows:
        for kind, size in parts:
            row = jnp.zeros((1, HDIM), F32)
            for b in range(blocks):
                if kind == BEYOND:
                    seen = (frame > 0) & (frame < frames - 1)
                elif kind != PAIR:
                    seen = mask_ref[0, b, kind] > 0
                else:
                    continue
                row = jnp.where(lane == b, jnp.where(seen, 0.0, MASKED), row)
            pieces.append(jnp.broadcast_to(row, (size, HDIM)).astype(BF16))
    return jnp.concatenate(pieces, axis=0)


def attend_kernel(head, heads, rows, aliased, mask_ref, *refs):
    count = len(rows)
    q_ref, g_ref, k_ref, v_ref = refs[:4]
    got = refs[4 : 4 + count]
    refs = refs[4 + count + aliased :]
    o_ref, dq_ref, own_ref = refs[:3]
    back = refs[3 : 3 + count]
    keys, vals = refs[3 + count :]
    tokens = q_ref.shape[0]
    blocks = tokens // BLK
    bias = bias_columns(mask_ref, tokens, blocks, rows)
    for slot in range(2):
        keys[slot, :, HDIM:] = bias
    block = lax.broadcasted_iota(jnp.int32, (tokens, HDIM), 0) // BLK
    lane = lax.broadcasted_iota(jnp.int32, (tokens, HDIM), 1)
    choose = jnp.where(lane == block, 1.0, 0.0).astype(BF16)

    def column(h, ref):
        return pl.ds((h if ref.shape[-1] == heads * HDIM else head + h) * HDIM, HDIM)

    def products(h):
        at = 0
        slot = h % 2
        for ref in (k_ref, v_ref):
            half = keys.at[slot, :, :HDIM] if ref is k_ref else vals.at[slot]
            half[0:tokens] = ref[:, column(h, ref)]
        at = tokens
        for ref in got:
            size = ref.shape[1]
            keys[slot, at : at + size, :HDIM] = ref[0, :, column(h, ref)]
            vals[slot, at : at + size] = ref[1, :, column(h, ref)]
            at += size
        query = jnp.concatenate([q_ref[:, column(h, q_ref)], choose], axis=1)
        return dot(query, keys[slot], NT), dot(g_ref[:, column(h, g_ref)], vals[slot], NT)

    ahead = products(0)
    for h in range(heads):
        scores, dprob = ahead
        if h + 1 < heads:
            ahead = products(h + 1)
        scores = scores * (SCALE * LOG2E)
        weights = jnp.exp2(scores - jnp.max(scores, axis=1, keepdims=True))
        weights = weights * (1.0 / jnp.sum(weights, axis=1, keepdims=True))
        rounded = weights.astype(BF16)
        inner = jnp.sum(weights * dprob, axis=1, keepdims=True)
        dscore = (weights * (dprob - inner)).astype(BF16)
        slot = h % 2
        query, grad = q_ref[:, column(h, q_ref)], g_ref[:, column(h, g_ref)]
        o_ref[:, column(h, o_ref)] = dot(rounded, vals[slot]).astype(BF16)
        dq_ref[:, column(h, dq_ref)] = (dot(dscore, keys[slot, :, :HDIM]) * SCALE).astype(BF16)
        for side, term in enumerate((dot(dscore, query, TN) * SCALE, dot(rounded, grad, TN))):
            own_ref[side, :, column(h, own_ref)] = term[:tokens]
            at = tokens
            for ref in back:
                size = ref.shape[1]
                ref[side, :, column(h, ref)] = term[at : at + size].astype(BF16)
                at += size


def attend(mask, queries, out_grad, keys, values, got, rows, previous, head, heads):
    tokens, feat = queries.shape
    width = heads * HDIM
    sizes = [piece.shape[1] for piece in got]
    total = tokens + sum(sizes)
    inputs = vmem((queries, out_grad, keys, values, *got))
    aliases = {}
    if previous is not None:
        aliases = {1 + len(inputs): 0, 2 + len(inputs): 1}
        inputs += vmem(previous)
    whole = pl.BlockSpec(memory_space=pltpu.VMEM)
    out_shape = [pltpu.VMEM((tokens, feat), BF16)] * 2 + [pltpu.VMEM((2, tokens, width), F32)]
    out_shape += [pltpu.VMEM((2, size, width), BF16) for size in sizes]
    return pl.pallas_call(
        functools.partial(attend_kernel, head, heads, rows, len(aliases)),
        out_shape=out_shape,
        in_specs=[pl.BlockSpec(memory_space=pltpu.SMEM)] + [whole] * len(inputs),
        out_specs=[whole] * len(out_shape),
        scratch_shapes=[
            pltpu.VMEM((2, total, 2 * HDIM), BF16),
            pltpu.VMEM((2, total, HDIM), BF16),
        ],
        input_output_aliases=aliases,
        compiler_params=pltpu.CompilerParams(vmem_limit_bytes=24 << 20),
        cost_estimate=cost(
            12 * tokens * total * width,
            2 * width * (6 * tokens + 4 * tokens + 4 * (total - tokens)),
            tokens * total * heads,
        ),
    )(mask, *inputs)


def combine_kernel(head, heads, rows, aliased, pick_ref, own_ref, *refs):
    got = refs[: len(rows)]
    refs = refs[len(rows) + aliased :]
    outs, acc, done, sem = refs[:2], refs[2], refs[3], refs[4]
    tokens = own_ref.shape[1]
    starts = [[start_of(kind, pick_ref, tokens) for kind, _ in parts] for parts in rows]
    copies = []
    for side in range(2):
        acc[...] = own_ref[side]
        for ref, parts, spots in zip(got, rows, starts, strict=True):
            at = 0
            cut = slice(None) if ref.shape[2] == heads * HDIM else slice(head * HDIM, (head + heads) * HDIM)
            for (_, size), start in zip(parts, spots, strict=True):
                acc[pl.ds(start, size)] += ref[side, at : at + size, cut].astype(F32)
                at += size
        done[side] = acc[...].astype(BF16)
        target = outs[side].at[:, pl.ds(head * HDIM, heads * HDIM)]
        copies.append(pltpu.make_async_copy(done.at[side], target, sem.at[side]))
        copies[-1].start()
    for copy in copies:
        copy.wait()


def combine(picks, own, got, rows, previous, head, heads, feat):
    tokens = own.shape[1]
    inputs = vmem((own, *got))
    specs = [pl.BlockSpec(memory_space=pltpu.VMEM)] * len(inputs)
    aliases = {}
    if previous is not None:
        aliases = {1 + len(inputs): 0, 2 + len(inputs): 1}
        inputs += hbm(previous)
        specs += [ANY, ANY]
    return pl.pallas_call(
        functools.partial(combine_kernel, head, heads, rows, len(aliases)),
        out_shape=[pltpu.HBM((tokens, feat), BF16)] * 2,
        in_specs=[pl.BlockSpec(memory_space=pltpu.SMEM)] + specs,
        out_specs=[ANY, ANY],
        scratch_shapes=[
            pltpu.VMEM((tokens, heads * HDIM), F32),
            pltpu.VMEM((2, tokens, heads * HDIM), BF16),
            pltpu.SemaphoreType.DMA((2,)),
        ],
        input_output_aliases=aliases,
        compiler_params=pltpu.CompilerParams(vmem_limit_bytes=8 << 20),
        cost_estimate=cost(0, 8 * own.size),
    )(picks, *inputs)


def after(pieces, results):
    return [lax.optimization_barrier((piece, *results))[0] for piece in pieces]


def per_device(queries, key_rows, value_rows, out_grad, block_mask, block_pick):
    frames = lax.axis_size("frame")
    levels = frames.bit_length() - 1
    feat = queries.shape[1]
    mask = jnp.swapaxes(block_mask, 1, 2)
    rows = [[(level, BLK)] for level in range(levels - 1, 0, -1)]
    rows += [[(0, BLK), (PAIR, EDGE)], [(BEYOND, EDGE)]]
    pairs = [[(f, f ^ (1 << level)) for f in range(frames)] for level in range(levels - 1, -1, -1)]
    beyond = [f + (1 if f % 2 else -1) for f in range(frames)]
    pairs.append([(f, g if 0 <= g < frames else f) for f, g in enumerate(beyond)])

    def send(pieces, to):
        return [lax.ppermute(piece, "frame", t) for piece, t in zip(pieces, to, strict=True)]

    far = len(rows) - 2
    heads_at = [sum(SPLIT[:i]) for i in range(len(SPLIT))]
    chunks = list(zip(heads_at, SPLIT, strict=True))
    cuts = [[(parts, at * HDIM, n * HDIM) for parts in rows[:far]] for at, n in chunks]
    return_gates = [[0]] + [[]] * (far - 1) + [[0, 1, far + 1], [1, far - 1, far]]

    def gated(pieces, before, gates):
        return [
            lax.optimization_barrier((piece, *(before[i] for i in gate)))[0]
            for piece, gate in zip(pieces, gates, strict=True)
        ]

    whole = [(rows[far], 0, feat), (rows[far + 1], 0, feat)]
    *near, = pack(block_pick, key_rows, value_rows, whole + cuts[0])
    first = near[2:]
    edge = send(near[1:2], pairs[far + 1 :])
    fetched = [send(first, pairs[:far])]
    near = send(near[:1], pairs[far : far + 1])
    last = first[:1]
    for cut in cuts[1:]:
        *pieces, = pack(block_pick, *after((key_rows, value_rows), last), cut)
        last = pieces[:1]
        before = fetched[-1]
        gates = [[before[0], *near] for i in range(far)]
        pieces = [after([p], gate)[0] for p, gate in zip(pieces, gates, strict=True)]
        fetched.append(send(pieces, pairs[:far]))
    fetched = [got + near + edge for got in fetched]
    outs = None
    returned = []
    for (head, heads), got in zip(chunks, fetched, strict=True):
        attended, query_grad, own, *terms = attend(
            mask, queries, out_grad, key_rows, value_rows, got, rows, outs, head, heads
        )
        outs = (attended, query_grad)
        if returned:
            terms = gated(terms, returned[-1][1], return_gates)
        returned.append((own, send(terms, pairs)))
    grads = None
    for (head, heads), (own, got) in zip(chunks, returned, strict=True):
        grads = combine(block_pick, own, got, rows, grads, head, heads, feat)
    return (*outs, *grads)


def solution(mesh):
    flat = P(("group", "frame"), None)
    return jax.shard_map(
        per_device,
        mesh=mesh,
        in_specs=(flat, flat, flat, flat, P(("group", "frame"), None, None), flat),
        out_specs=(flat, flat, flat, flat),
        check_vma=False,
    )
```

profile of v0, /device:TPU:0, one launch (start us, length us, event | category | flops | bytes accessed | tf_op | source)
XLA Modules:
  0.0 91.1 jit_solution(5430296357926596876)
XLA Ops:
  0.6 0.0 copy-start.1
  0.7 0.8 copy-done.2
  1.4 2.4 %shard_map.93 = (bf16[2,192,1536]{2,1,0:T(8,128)(2,1)S(1)}, bf16[2,64,1536]{2,1,0:T(8,128)(2,1)S(1)}, bf16[2,128,768]{2,1,0:T(8,128)(2,1)S(1)}, bf16[2,128,768]{2,1,0:T(8,128)(2,1)S(1)}, bf16[2,128,768]{2,1,0:T(8,128)(2,1)S(1)}) custom-call(s32[1,4]{1,0:T(1,128)S(1)} %copy-done.2, bf16[256,1536]{1,0:T(8,128)(2,1)} %refs_2_.3, bf16[256,1536]{1,0:T(8,128)(2,1)} %refs_3_.3), custom_call_target="tpu_custom_call" | custom-call | bytes 5505024 | tf_op jit(solution)/shard_map/pallas_call | solution.py:76
  3.9 0.5 collective-permute-start.1
  4.4 4.1 %collective-permute-start = (bf16[2,128,768]{2,1,0:T(8,128)(2,1)S(1)}, bf16[2,128,768]{2,1,0:T(8,128)(2,1)S(1)}, u32[]{:S(2)}, u32[]{:S(2)}) collective-permute-start(bf16[2,128,768]{2,1,0:T(8,128)(2,1)S(1)} %get-tuple-element.40), channel_id=1, source_target_pairs={{0,8},{1,9},{2,10},{3,11},{4,12},{5,13},{6,14},{7,15},{8,0},{9,1},... | collective-permute-start | bytes 1179656 | tf_op jit(solution)/shard_map/ppermute | solution.py:266
  8.5 0.7 collective-permute-start.5
  9.2 3.5 %collective-permute-start.6 = (bf16[2,128,768]{2,1,0:T(8,128)(2,1)S(1)}, bf16[2,128,768]{2,1,0:T(8,128)(2,1)S(1)}, u32[]{:S(2)}, u32[]{:S(2)}) collective-permute-start(bf16[2,128,768]{2,1,0:T(8,128)(2,1)S(1)} %get-tuple-element.51), channel_id=1, source_target_pairs={{0,4},{1,5},{2,6},{3,7},{4,0},{5,1},{6,2},{7,3},{8,12},{9,13},{10,... | collective-permute-start | bytes 1179656 | tf_op jit(solution)/shard_map/ppermute | solution.py:266
  12.7 0.9 %collective-permute-start.7 = (bf16[2,128,768]{2,1,0:T(8,128)(2,1)S(1)}, bf16[2,128,768]{2,1,0:T(8,128)(2,1)S(1)}, u32[]{:S(2)}, u32[]{:S(2)}) collective-permute-start(bf16[2,128,768]{2,1,0:T(8,128)(2,1)S(1)} %get-tuple-element.52), channel_id=1, source_target_pairs={{0,2},{1,3},{2,0},{3,1},{4,6},{5,7},{6,4},{7,5},{8,10},{9,11},{10,... | collective-permute-start | bytes 1179656 | tf_op jit(solution)/shard_map/ppermute | solution.py:266
  13.6 2.0 %shard_map.94 = (bf16[2,128,768]{2,1,0:T(8,128)(2,1)S(1)}, bf16[2,128,768]{2,1,0:T(8,128)(2,1)S(1)}, bf16[2,128,768]{2,1,0:T(8,128)(2,1)S(1)}) custom-call(s32[1,4]{1,0:T(1,128)S(1)} %copy-done.3, bf16[256,1536]{1,0:T(8,128)(2,1)} %refs_2_.3, bf16[256,1536]{1,0:T(8,128)(2,1)} %refs_3_.3), custom_call_target="tpu_custom_call" | custom-call | bytes 2359296 | tf_op jit(solution)/shard_map/pallas_call | solution.py:76
  15.6 11.1 %collective-permute-done.refs_4_ = bf16[2,128,768]{2,1,0:T(8,128)(2,1)S(1)} collective-permute-done((bf16[2,128,768]{2,1,0:T(8,128)(2,1)S(1)}, bf16[2,128,768]{2,1,0:T(8,128)(2,1)S(1)}, u32[]{:S(2)}, u32[]{:S(2)}) %collective-permute-start) | collective-permute-done | bytes 393248 | tf_op jit(solution)/shard_map/ppermute | solution.py:266
  26.8 4.0 %collective-permute-start.3 = (bf16[2,128,768]{2,1,0:T(8,128)(2,1)S(1)}, bf16[2,128,768]{2,1,0:T(8,128)(2,1)S(1)}, u32[]{:S(2)}, u32[]{:S(2)}) collective-permute-start(bf16[2,128,768]{2,1,0:T(8,128)(2,1)S(1)} %get-tuple-element.47), channel_id=1, source_target_pairs={{0,4},{1,5},{2,6},{3,7},{4,0},{5,1},{6,2},{7,3},{8,12},{9,13},{10,... | collective-permute-start | bytes 1179656 | tf_op jit(solution)/shard_map/ppermute | solution.py:266
  30.8 1.1 %collective-permute-start.4 = (bf16[2,128,768]{2,1,0:T(8,128)(2,1)S(1)}, bf16[2,128,768]{2,1,0:T(8,128)(2,1)S(1)}, u32[]{:S(2)}, u32[]{:S(2)}) collective-permute-start(bf16[2,128,768]{2,1,0:T(8,128)(2,1)S(1)} %get-tuple-element.49), channel_id=1, source_target_pairs={{0,2},{1,3},{2,0},{3,1},{4,6},{5,7},{6,4},{7,5},{8,10},{9,11},{10,... | collective-permute-start | bytes 1179656 | tf_op jit(solution)/shard_map/ppermute | solution.py:266
  31.9 6.9 %collective-permute-done.6.refs_5_ = bf16[2,128,768]{2,1,0:T(8,128)(2,1)S(1)} collective-permute-done((bf16[2,128,768]{2,1,0:T(8,128)(2,1)S(1)}, bf16[2,128,768]{2,1,0:T(8,128)(2,1)S(1)}, u32[]{:S(2)}, u32[]{:S(2)}) %collective-permute-start.6) | collective-permute-done | bytes 393248 | tf_op jit(solution)/shard_map/ppermute | solution.py:266
  38.8 6.5 %shard_map.95 = (bf16[256,1536]{1,0:T(8,128)(2,1)S(1)}, bf16[256,1536]{1,0:T(8,128)(2,1)S(1)}, f32[2,256,768]{2,1,0:T(8,128)S(1)}, bf16[2,128,768]{2,1,0:T(8,128...) custom-call(s32[1,2,4]{2,1,0:T(2,128)S(1)} %bitcast.1, ...), custom_call_target="tpu_custom_call" | custom-call | flops 2113929216 | bytes 7864320 | tf_op jit(solution)/shard_map/pallas_call | solution.py:183
  45.3 3.2 %collective-permute-start.8 = (bf16[2,128,768]{2,1,0:T(8,128)(2,1)S(1)}, bf16[2,128,768]{2,1,0:T(8,128)(2,1)S(1)}, u32[]{:S(2)}, u32[]{:S(2)}) collective-permute-start(bf16[2,128,768]{2,1,0:T(8,128)(2,1)S(1)} %get-tuple-element.59), channel_id=1, source_target_pairs={{0,8},{1,9},{2,10},{3,11},{4,12},{5,13},{6,14},{7,15},{8,0},{9,1},... | collective-permute-start | bytes 1179656 | tf_op jit(solution)/shard_map/ppermute | solution.py:266
  48.5 0.1 collective-permute-done.2.refs_4_
  48.7 0.8 collective-permute-start.13
  49.5 6.0 %collective-permute-done.3.refs_5_ = bf16[2,128,768]{2,1,0:T(8,128)(2,1)S(1)} collective-permute-done((bf16[2,128,768]{2,1,0:T(8,128)(2,1)S(1)}, bf16[2,128,768]{2,1,0:T(8,128)(2,1)S(1)}, u32[]{:S(2)}, u32[]{:S(2)}) %collective-permute-start.3) | collective-permute-done | bytes 393248 | tf_op jit(solution)/shard_map/ppermute | solution.py:266
  55.5 3.7 %collective-permute-start.15 = (bf16[2,128,768]{2,1,0:T(8,128)(2,1)S(1)}, bf16[2,128,768]{2,1,0:T(8,128)(2,1)S(1)}, u32[]{:S(2)}, u32[]{:S(2)}) collective-permute-start(bf16[2,128,768]{2,1,0:T(8,128)(2,1)S(1)} %get-tuple-element.68), channel_id=1, source_target_pairs={{0,2},{1,3},{2,0},{3,1},{4,6},{5,7},{6,4},{7,5},{8,10},{9,11},{10,... | collective-permute-start | bytes 1179656 | tf_op jit(solution)/shard_map/ppermute | solution.py:266
  59.2 0.2 collective-permute-start.16
  59.4 6.4 %shard_map.96 = (bf16[256,1536]{1,0:T(8,128)(2,1)S(1)}, bf16[256,1536]{1,0:T(8,128)(2,1)S(1)}, f32[2,256,768]{2,1,0:T(8,128)S(1)}, bf16[2,128,768]{2,1,0:T(8,128...) custom-call(s32[1,2,4]{2,1,0:T(2,128)S(1)} %bitcast.2, ...), custom_call_target="tpu_custom_call", output_to_operand_aliasing={{0}: (10, {}), {1}: (11, {})} | custom-call | flops 2113929216 | bytes 7864320 | tf_op jit(solution)/shard_map/pallas_call | solution.py:183
  65.9 2.1 %collective-permute-done.12.refs_1_ = bf16[2,128,768]{2,1,0:T(8,128)(2,1)S(1)} collective-permute-done((bf16[2,128,768]{2,1,0:T(8,128)(2,1)S(1)}, bf16[2,128,768]{2,1,0:T(8,128)(2,1)S(1)}, u32[]{:S(2)}, u32[]{:S(2)}) %collective-permute-start.12) | collective-permute-done | bytes 393248 | tf_op jit(solution)/shard_map/ppermute | solution.py:266
  68.0 2.0 %collective-permute-start.9 = (bf16[2,128,768]{2,1,0:T(8,128)(2,1)S(1)}, bf16[2,128,768]{2,1,0:T(8,128)(2,1)S(1)}, u32[]{:S(2)}, u32[]{:S(2)}) collective-permute-start(bf16[2,128,768]{2,1,0:T(8,128)(2,1)S(1)} %get-tuple-element.60), channel_id=1, source_target_pairs={{0,8},{1,9},{2,10},{3,11},{4,12},{5,13},{6,14},{7,15},{8,0},{9,1},... | collective-permute-start | bytes 1179656 | tf_op jit(solution)/shard_map/ppermute | solution.py:266
  70.0 2.9 %collective-permute-start.10 = (bf16[2,128,768]{2,1,0:T(8,128)(2,1)S(1)}, bf16[2,128,768]{2,1,0:T(8,128)(2,1)S(1)}, u32[]{:S(2)}, u32[]{:S(2)}) collective-permute-start(bf16[2,128,768]{2,1,0:T(8,128)(2,1)S(1)} %get-tuple-element.61), channel_id=1, source_target_pairs={{0,4},{1,5},{2,6},{3,7},{4,0},{5,1},{6,2},{7,3},{8,12},{9,13},{10,... | collective-permute-start | bytes 1179656 | tf_op jit(solution)/shard_map/ppermute | solution.py:266
  72.8 0.4 collective-permute-start.11
  73.3 0.7 collective-permute-start.17
  74.0 0.9 copy.18
  74.8 0.9 copy.19
  75.7 1.9 %shard_map.97 = (bf16[256,1536]{1,0:T(8,128)(2,1)}, bf16[256,1536]{1,0:T(8,128)(2,1)}) custom-call(s32[1,4]{1,0:T(1,128)S(1)} %copy-done.3, f32[2,256,768]{2,1,0:T(8,128)S(1)} %get-tuple-element.71.own_ref, bf16[2,128,768]{2,1,0:T(8,128)(2,1)S(1)} %collective-permute-done.8.refs_0_, bf16[2,128,768]{2,1,0:T(8,128)(2,1)S(1)} %collective-permute-done.12.refs_1_, ...), custom_call_target="tpu_custom_call" | custom-call | bytes 3145728 | tf_op jit(solution)/shard_map/pallas_call | solution.py:234
  77.6 11.4 %collective-permute-done.9.refs_0_ = bf16[2,128,768]{2,1,0:T(8,128)(2,1)S(1)} collective-permute-done((bf16[2,128,768]{2,1,0:T(8,128)(2,1)S(1)}, bf16[2,128,768]{2,1,0:T(8,128)(2,1)S(1)}, u32[]{:S(2)}, u32[]{:S(2)}) %collective-permute-start.9) | collective-permute-done | bytes 393248 | tf_op jit(solution)/shard_map/ppermute | solution.py:266
  89.0 0.1 collective-permute-done.10.refs_1_
  89.1 1.9 %shard_map.98 = (bf16[256,1536]{1,0:T(8,128)(2,1)}, bf16[256,1536]{1,0:T(8,128)(2,1)}) custom-call(s32[1,4]{1,0:T(1,128)S(1)} %copy-done.3, f32[2,256,768]{2,1,0:T(8,128)S(1)} %get-tuple-element.57.own_ref, bf16[2,128,768]{2,1,0:T(8,128)(2,1)S(1)} %collective-permute-done.9.refs_0_, ...), custom_call_target="tpu_custom_call", output_to_operand_aliasing={{0}: (7, {}), {1}: (8, {})} | custom-call | bytes 3145728 | tf_op jit(solution)/shard_map/pallas_call | solution.py:234
  (26 shorter events, 0.1 us)
Async XLA Ops:
  0.6 38.2 %copy-start.1 = (bf16[256,1536]{1,0:T(8,128)(2,1)S(1)}, bf16[256,1536]{1,0:T(8,128)(2,1)}, u32[]{:S(2)}) copy-start(bf16[256,1536]{1,0:T(8,128)(2,1)} %refs_3_.3) | copy-start | bytes 2359300
  0.6 38.1 %copy-start = (bf16[256,1536]{1,0:T(8,128)(2,1)S(1)}, bf16[256,1536]{1,0:T(8,128)(2,1)}, u32[]{:S(2)}) copy-start(bf16[256,1536]{1,0:T(8,128)(2,1)} %refs_2_.3) | copy-start | bytes 2359300
  0.7 0.8 copy-start.2
  1.4 12.2 %copy-start.3 = (s32[1,4]{1,0:T(1,128)S(1)}, s32[1,4]{1,0:T(1,128)}, u32[]{:S(2)}) copy-start(s32[1,4]{1,0:T(1,128)} %pick_ref.7) | copy-start | bytes 52
  1.4 37.4 %copy-start.4 = (bf16[256,1536]{1,0:T(8,128)(2,1)S(1)}, bf16[256,1536]{1,0:T(8,128)(2,1)}, u32[]{:S(2)}) copy-start(bf16[256,1536]{1,0:T(8,128)(2,1)} %refs_0_.3) | copy-start | bytes 2359300
  1.4 37.4 %copy-start.5 = (bf16[256,1536]{1,0:T(8,128)(2,1)S(1)}, bf16[256,1536]{1,0:T(8,128)(2,1)}, u32[]{:S(2)}) copy-start(bf16[256,1536]{1,0:T(8,128)(2,1)} %refs_1_.3) | copy-start | bytes 2359300
  1.4 37.4 %copy-start.6 = (s32[1,4,2]{1,2,0:T(2,128)S(1)}, s32[1,4,2]{1,2,0:T(2,128)}, u32[]{:S(2)}) copy-start(s32[1,4,2]{1,2,0:T(2,128)} %param.10) | copy-start | bytes 100
  3.9 22.9 %collective-permute-start.1 = (bf16[2,192,1536]{2,1,0:T(8,128)(2,1)S(1)}, bf16[2,192,1536]{2,1,0:T(8,128)(2,1)S(1)}, u32[]{:S(2)}, u32[]{:S(2)}) collective-permute-start(bf16[2,192,1536]{2,1,0:T(8,128)(2,1)S(1)} %get-tuple-element.44), channel_id=1, source_target_pairs={{0,1},{1,0},{2,3},{3,2},{4,5},{5,4},{6,7},{7,6},{8,9},{9,8},{10,11... | collective-permute-start | bytes 3538952 | tf_op jit(solution)/shard_map/ppermute | solution.py:266
  4.4 22.4 %collective-permute-start = (bf16[2,128,768]{2,1,0:T(8,128)(2,1)S(1)}, bf16[2,128,768]{2,1,0:T(8,128)(2,1)S(1)}, u32[]{:S(2)}, u32[]{:S(2)}) collective-permute-start(bf16[2,128,768]{2,1,0:T(8,128)(2,1)S(1)} %get-tuple-element.40), channel_id=1, source_target_pairs={{0,8},{1,9},{2,10},{3,11},{4,12},{5,13},{6,14},{7,15},{8,0},{9,1},... | collective-permute-start | bytes 1179656 | tf_op jit(solution)/shard_map/ppermute | solution.py:266
  8.5 22.3 %collective-permute-start.5 = (bf16[2,64,1536]{2,1,0:T(8,128)(2,1)S(1)}, bf16[2,64,1536]{2,1,0:T(8,128)(2,1)S(1)}, u32[]{:S(2)}, u32[]{:S(2)}) collective-permute-start(bf16[2,64,1536]{2,1,0:T(8,128)(2,1)S(1)} %get-tuple-element.50), channel_id=1, source_target_pairs={{0,0},{1,2},{2,1},{3,4},{4,3},{5,6},{6,5},{7,8},{8,7},{9,10},{10,9... | collective-permute-start | bytes 1179656 | tf_op jit(solution)/shard_map/ppermute | solution.py:266
  9.2 29.6 %collective-permute-start.6 = (bf16[2,128,768]{2,1,0:T(8,128)(2,1)S(1)}, bf16[2,128,768]{2,1,0:T(8,128)(2,1)S(1)}, u32[]{:S(2)}, u32[]{:S(2)}) collective-permute-start(bf16[2,128,768]{2,1,0:T(8,128)(2,1)S(1)} %get-tuple-element.51), channel_id=1, source_target_pairs={{0,4},{1,5},{2,6},{3,7},{4,0},{5,1},{6,2},{7,3},{8,12},{9,13},{10,... | collective-permute-start | bytes 1179656 | tf_op jit(solution)/shard_map/ppermute | solution.py:266
  12.7 26.1 %collective-permute-start.7 = (bf16[2,128,768]{2,1,0:T(8,128)(2,1)S(1)}, bf16[2,128,768]{2,1,0:T(8,128)(2,1)S(1)}, u32[]{:S(2)}, u32[]{:S(2)}) collective-permute-start(bf16[2,128,768]{2,1,0:T(8,128)(2,1)S(1)} %get-tuple-element.52), channel_id=1, source_target_pairs={{0,2},{1,3},{2,0},{3,1},{4,6},{5,7},{6,4},{7,5},{8,10},{9,11},{10,... | collective-permute-start | bytes 1179656 | tf_op jit(solution)/shard_map/ppermute | solution.py:266
  26.8 21.9 %collective-permute-start.2 = (bf16[2,128,768]{2,1,0:T(8,128)(2,1)S(1)}, bf16[2,128,768]{2,1,0:T(8,128)(2,1)S(1)}, u32[]{:S(2)}, u32[]{:S(2)}) collective-permute-start(bf16[2,128,768]{2,1,0:T(8,128)(2,1)S(1)} %get-tuple-element.45), channel_id=1, source_target_pairs={{0,8},{1,9},{2,10},{3,11},{4,12},{5,13},{6,14},{7,15},{8,0},{9,1},... | collective-permute-start | bytes 1179656 | tf_op jit(solution)/shard_map/ppermute | solution.py:266
  26.8 28.7 %collective-permute-start.3 = (bf16[2,128,768]{2,1,0:T(8,128)(2,1)S(1)}, bf16[2,128,768]{2,1,0:T(8,128)(2,1)S(1)}, u32[]{:S(2)}, u32[]{:S(2)}) collective-permute-start(bf16[2,128,768]{2,1,0:T(8,128)(2,1)S(1)} %get-tuple-element.47), channel_id=1, source_target_pairs={{0,4},{1,5},{2,6},{3,7},{4,0},{5,1},{6,2},{7,3},{8,12},{9,13},{10,... | collective-permute-start | bytes 1179656 | tf_op jit(solution)/shard_map/ppermute | solution.py:266
  30.8 28.4 %collective-permute-start.4 = (bf16[2,128,768]{2,1,0:T(8,128)(2,1)S(1)}, bf16[2,128,768]{2,1,0:T(8,128)(2,1)S(1)}, u32[]{:S(2)}, u32[]{:S(2)}) collective-permute-start(bf16[2,128,768]{2,1,0:T(8,128)(2,1)S(1)} %get-tuple-element.49), channel_id=1, source_target_pairs={{0,2},{1,3},{2,0},{3,1},{4,6},{5,7},{6,4},{7,5},{8,10},{9,11},{10,... | collective-permute-start | bytes 1179656 | tf_op jit(solution)/shard_map/ppermute | solution.py:266
  45.3 20.6 %collective-permute-start.8 = (bf16[2,128,768]{2,1,0:T(8,128)(2,1)S(1)}, bf16[2,128,768]{2,1,0:T(8,128)(2,1)S(1)}, u32[]{:S(2)}, u32[]{:S(2)}) collective-permute-start(bf16[2,128,768]{2,1,0:T(8,128)(2,1)S(1)} %get-tuple-element.59), channel_id=1, source_target_pairs={{0,8},{1,9},{2,10},{3,11},{4,12},{5,13},{6,14},{7,15},{8,0},{9,1},... | collective-permute-start | bytes 1179656 | tf_op jit(solution)/shard_map/ppermute | solution.py:266
  48.5 19.5 %collective-permute-start.12 = (bf16[2,128,768]{2,1,0:T(8,128)(2,1)S(1)}, bf16[2,128,768]{2,1,0:T(8,128)(2,1)S(1)}, u32[]{:S(2)}, u32[]{:S(2)}) collective-permute-start(bf16[2,128,768]{2,1,0:T(8,128)(2,1)S(1)} %get-tuple-element.64), channel_id=1, source_target_pairs={{0,4},{1,5},{2,6},{3,7},{4,0},{5,1},{6,2},{7,3},{8,12},{9,13},{10,... | collective-permute-start | bytes 1179656 | tf_op jit(solution)/shard_map/ppermute | solution.py:266
  48.7 17.2 %collective-permute-start.13 = (bf16[2,64,768]{2,1,0:T(8,128)(2,1)S(1)}, bf16[2,64,768]{2,1,0:T(8,128)(2,1)S(1)}, u32[]{:S(2)}, u32[]{:S(2)}) collective-permute-start(bf16[2,64,768]{2,1,0:T(8,128)(2,1)S(1)} %get-tuple-element.65), channel_id=1, source_target_pairs={{0,0},{1,2},{2,1},{3,4},{4,3},{5,6},{6,5},{7,8},{8,7},{9,10},{10,9... | collective-permute-start | bytes 589832 | tf_op jit(solution)/shard_map/ppermute | solution.py:266
  55.5 17.4 %collective-permute-start.15 = (bf16[2,128,768]{2,1,0:T(8,128)(2,1)S(1)}, bf16[2,128,768]{2,1,0:T(8,128)(2,1)S(1)}, u32[]{:S(2)}, u32[]{:S(2)}) collective-permute-start(bf16[2,128,768]{2,1,0:T(8,128)(2,1)S(1)} %get-tuple-element.68), channel_id=1, source_target_pairs={{0,2},{1,3},{2,0},{3,1},{4,6},{5,7},{6,4},{7,5},{8,10},{9,11},{10,... | collective-permute-start | bytes 1179656 | tf_op jit(solution)/shard_map/ppermute | solution.py:266
  59.2 14.1 %collective-permute-start.16 = (bf16[2,192,768]{2,1,0:T(8,128)(2,1)S(1)}, bf16[2,192,768]{2,1,0:T(8,128)(2,1)S(1)}, u32[]{:S(2)}, u32[]{:S(2)}) collective-permute-start(bf16[2,192,768]{2,1,0:T(8,128)(2,1)S(1)} %get-tuple-element.69), channel_id=1, source_target_pairs={{0,1},{1,0},{2,3},{3,2},{4,5},{5,4},{6,7},{7,6},{8,9},{9,8},{10,11... | collective-permute-start | bytes 1769480 | tf_op jit(solution)/shard_map/ppermute | solution.py:266
  68.0 21.0 %collective-permute-start.14 = (bf16[2,192,768]{2,1,0:T(8,128)(2,1)S(1)}, bf16[2,192,768]{2,1,0:T(8,128)(2,1)S(1)}, u32[]{:S(2)}, u32[]{:S(2)}) collective-permute-start(bf16[2,192,768]{2,1,0:T(8,128)(2,1)S(1)} %get-tuple-element.66), channel_id=1, source_target_pairs={{0,1},{1,0},{2,3},{3,2},{4,5},{5,4},{6,7},{7,6},{8,9},{9,8},{10,11... | collective-permute-start | bytes 1769480 | tf_op jit(solution)/shard_map/ppermute | solution.py:266
  68.0 21.0 %collective-permute-start.9 = (bf16[2,128,768]{2,1,0:T(8,128)(2,1)S(1)}, bf16[2,128,768]{2,1,0:T(8,128)(2,1)S(1)}, u32[]{:S(2)}, u32[]{:S(2)}) collective-permute-start(bf16[2,128,768]{2,1,0:T(8,128)(2,1)S(1)} %get-tuple-element.60), channel_id=1, source_target_pairs={{0,8},{1,9},{2,10},{3,11},{4,12},{5,13},{6,14},{7,15},{8,0},{9,1},... | collective-permute-start | bytes 1179656 | tf_op jit(solution)/shard_map/ppermute | solution.py:266
  70.0 19.1 %collective-permute-start.10 = (bf16[2,128,768]{2,1,0:T(8,128)(2,1)S(1)}, bf16[2,128,768]{2,1,0:T(8,128)(2,1)S(1)}, u32[]{:S(2)}, u32[]{:S(2)}) collective-permute-start(bf16[2,128,768]{2,1,0:T(8,128)(2,1)S(1)} %get-tuple-element.61), channel_id=1, source_target_pairs={{0,4},{1,5},{2,6},{3,7},{4,0},{5,1},{6,2},{7,3},{8,12},{9,13},{10,... | collective-permute-start | bytes 1179656 | tf_op jit(solution)/shard_map/ppermute | solution.py:266
  72.8 16.2 %collective-permute-start.11 = (bf16[2,128,768]{2,1,0:T(8,128)(2,1)S(1)}, bf16[2,128,768]{2,1,0:T(8,128)(2,1)S(1)}, u32[]{:S(2)}, u32[]{:S(2)}) collective-permute-start(bf16[2,128,768]{2,1,0:T(8,128)(2,1)S(1)} %get-tuple-element.62), channel_id=1, source_target_pairs={{0,2},{1,3},{2,0},{3,1},{4,6},{5,7},{6,4},{7,5},{8,10},{9,11},{10,... | collective-permute-start | bytes 1179656 | tf_op jit(solution)/shard_map/ppermute | solution.py:266
  73.3 4.3 %collective-permute-start.17 = (bf16[2,64,768]{2,1,0:T(8,128)(2,1)S(1)}, bf16[2,64,768]{2,1,0:T(8,128)(2,1)S(1)}, u32[]{:S(2)}, u32[]{:S(2)}) collective-permute-start(bf16[2,64,768]{2,1,0:T(8,128)(2,1)S(1)} %get-tuple-element.70), channel_id=1, source_target_pairs={{0,0},{1,2},{2,1},{3,4},{4,3},{5,6},{6,5},{7,8},{8,7},{9,10},{10,9... | collective-permute-start | bytes 589832 | tf_op jit(solution)/shard_map/ppermute | solution.py:266
where the time goes:
time: 92.4 us; the launch traced here: 91.1 us
  waiting for transfers between devices  37.8 us (41%)
  starting transfers between devices  28.8 us (31%)
  Pallas kernels  21 us (23%)
  local copies, waits for them, and re-layouts  2.55 us (3%)
  between operations  0.95 us (1%)
    ppermute x18, waiting for transfers between devices, send(): lax.ppermute(piece, 'frame', t)  37.8 us
    ppermute x18, starting transfers between devices, send(): lax.ppermute(piece, 'frame', t)  28.8 us
    pallas_call x2, Pallas kernels, attend(): pl.pallas_call(functools.partial(attend_kernel, head, heads, rows, len(al...  12.9 us
    pallas_call x2, Pallas kernels, pack(): pl.pallas_call(functools.partial(pack_kernel, pieces), out_shape=[pltpu.V...  4.39 us
    pallas_call x2, Pallas kernels, combine(): pl.pallas_call(functools.partial(combine_kernel, head, heads, rows, len(a...  3.74 us
    unnamed x16, local copies, waits for them, and re-layouts  2.55 us
  transfers between devices with their start and end apart: 18, of which 7 were waited for; matrix products, arithmetic and copies ran while one was open for 2% of the time, Pallas kernels for 18%

commit v1 on v0

--- a/solution.py
+++ b/solution.py
@@ -269,7 +269,7 @@
     heads_at = [sum(SPLIT[:i]) for i in range(len(SPLIT))]
     chunks = list(zip(heads_at, SPLIT, strict=True))
     cuts = [[(parts, at * HDIM, n * HDIM) for parts in rows[:far]] for at, n in chunks]
-    return_gates = [[0]] + [[]] * (far - 1) + [[0, 1, far + 1], [1, far - 1, far]]
+    return_gates = [[]] * far + [[far], [*range(far + 1)]]
 
     def gated(pieces, before, gates):
         return [

time: 92.4 us -> 90.4 us (0.978)
  starting transfers between devices: 28.8 us -> 22.5 us
  waiting for transfers between devices: 37.8 us -> 41.9 us
    ppermute x18, starting transfers between devices: 28.8 us -> 22.5 us  [send(): lax.ppermute(piece, 'frame', t)]
    ppermute x18, waiting for transfers between devices: 37.8 us -> 41.9 us  [send(): lax.ppermute(piece, 'frame', t)]
  transfers between devices with their start and end apart: 18 -> 18, of which waited for: 7 -> 7; matrix products, arithmetic and copies ran while one was open for 2% -> 2% of each run, Pallas kernels for 18% -> 19%
where the time goes in v1:
time: 90.4 us; the launch traced here: 89.1 us
  waiting for transfers between devices  41.9 us (46%)
  starting transfers between devices  22.5 us (25%)
  Pallas kernels  21.3 us (24%)
  local copies, waits for them, and re-layouts  2.55 us (3%)
    ppermute x18, waiting for transfers between devices, send(): lax.ppermute(piece, 'frame', t)  41.9 us
    ppermute x18, starting transfers between devices, send(): lax.ppermute(piece, 'frame', t)  22.5 us
    pallas_call x2, Pallas kernels, attend(): pl.pallas_call(functools.partial(attend_kernel, head, heads, rows, len(al...  13 us
    pallas_call x2, Pallas kernels, pack(): pl.pallas_call(functools.partial(pack_kernel, pieces), out_shape=[pltpu.V...  4.55 us
    pallas_call x2, Pallas kernels, combine(): pl.pallas_call(functools.partial(combine_kernel, head, heads, rows, len(a...  3.74 us
    unnamed x16, local copies, waits for them, and re-layouts  2.55 us
  transfers between devices with their start and end apart: 18, of which 7 were waited for; matrix products, arithmetic and copies ran while one was open for 2% of the time, Pallas kernels for 19%

profile of v1, /device:TPU:0, one launch (start us, length us, event | category | flops | bytes accessed | tf_op | source)
XLA Modules:
  0.0 89.1 jit_solution(15533413192857856571)
XLA Ops:
  0.6 0.0 copy-start.1
  0.6 0.0 copy-start
  0.7 0.8 copy-done.2
  1.4 2.6 %shard_map.93 = (bf16[2,192,1536]{2,1,0:T(8,128)(2,1)S(1)}, bf16[2,64,1536]{2,1,0:T(8,128)(2,1)S(1)}, bf16[2,128,768]{2,1,0:T(8,128)(2,1)S(1)}, bf16[2,128,768]{2,1,0:T(8,128)(2,1)S(1)}, bf16[2,128,768]{2,1,0:T(8,128)(2,1)S(1)}) custom-call(s32[1,4]{1,0:T(1,128)S(1)} %copy-done.2, bf16[256,1536]{1,0:T(8,128)(2,1)} %refs_2_.3, bf16[256,1536]{1,0:T(8,128)(2,1)} %refs_3_.3), custom_call_target="tpu_custom_call" | custom-call | bytes 5505024 | tf_op jit(solution)/shard_map/pallas_call | solution.py:76
  4.0 0.6 collective-permute-start.1
  4.6 3.5 %collective-permute-start = (bf16[2,128,768]{2,1,0:T(8,128)(2,1)S(1)}, bf16[2,128,768]{2,1,0:T(8,128)(2,1)S(1)}, u32[]{:S(2)}, u32[]{:S(2)}) collective-permute-start(bf16[2,128,768]{2,1,0:T(8,128)(2,1)S(1)} %get-tuple-element.39), channel_id=1, source_target_pairs={{0,8},{1,9},{2,10},{3,11},{4,12},{5,13},{6,14},{7,15},{8,0},{9,1},... | collective-permute-start | bytes 1179656 | tf_op jit(solution)/shard_map/ppermute | solution.py:266
  8.2 0.7 collective-permute-start.5
  8.9 3.9 %collective-permute-start.6 = (bf16[2,128,768]{2,1,0:T(8,128)(2,1)S(1)}, bf16[2,128,768]{2,1,0:T(8,128)(2,1)S(1)}, u32[]{:S(2)}, u32[]{:S(2)}) collective-permute-start(bf16[2,128,768]{2,1,0:T(8,128)(2,1)S(1)} %get-tuple-element.50), channel_id=1, source_target_pairs={{0,4},{1,5},{2,6},{3,7},{4,0},{5,1},{6,2},{7,3},{8,12},{9,13},{10,... | collective-permute-start | bytes 1179656 | tf_op jit(solution)/shard_map/ppermute | solution.py:266
  12.8 0.6 collective-permute-start.7
  13.4 2.0 %shard_map.94 = (bf16[2,128,768]{2,1,0:T(8,128)(2,1)S(1)}, bf16[2,128,768]{2,1,0:T(8,128)(2,1)S(1)}, bf16[2,128,768]{2,1,0:T(8,128)(2,1)S(1)}) custom-call(s32[1,4]{1,0:T(1,128)S(1)} %copy-done.3, bf16[256,1536]{1,0:T(8,128)(2,1)} %refs_2_.3, bf16[256,1536]{1,0:T(8,128)(2,1)} %refs_3_.3), custom_call_target="tpu_custom_call" | custom-call | bytes 2359296 | tf_op jit(solution)/shard_map/pallas_call | solution.py:76
  15.4 10.9 %collective-permute-done.refs_4_ = bf16[2,128,768]{2,1,0:T(8,128)(2,1)S(1)} collective-permute-done((bf16[2,128,768]{2,1,0:T(8,128)(2,1)S(1)}, bf16[2,128,768]{2,1,0:T(8,128)(2,1)S(1)}, u32[]{:S(2)}, u32[]{:S(2)}) %collective-permute-start) | collective-permute-done | bytes 393248 | tf_op jit(solution)/shard_map/ppermute | solution.py:266
  26.3 4.1 %collective-permute-start.3 = (bf16[2,128,768]{2,1,0:T(8,128)(2,1)S(1)}, bf16[2,128,768]{2,1,0:T(8,128)(2,1)S(1)}, u32[]{:S(2)}, u32[]{:S(2)}) collective-permute-start(bf16[2,128,768]{2,1,0:T(8,128)(2,1)S(1)} %get-tuple-element.46), channel_id=1, source_target_pairs={{0,4},{1,5},{2,6},{3,7},{4,0},{5,1},{6,2},{7,3},{8,12},{9,13},{10,... | collective-permute-start | bytes 1179656 | tf_op jit(solution)/shard_map/ppermute | solution.py:266
  30.4 1.5 %collective-permute-start.4 = (bf16[2,128,768]{2,1,0:T(8,128)(2,1)S(1)}, bf16[2,128,768]{2,1,0:T(8,128)(2,1)S(1)}, u32[]{:S(2)}, u32[]{:S(2)}) collective-permute-start(bf16[2,128,768]{2,1,0:T(8,128)(2,1)S(1)} %get-tuple-element.48), channel_id=1, source_target_pairs={{0,2},{1,3},{2,0},{3,1},{4,6},{5,7},{6,4},{7,5},{8,10},{9,11},{10,... | collective-permute-start | bytes 1179656 | tf_op jit(solution)/shard_map/ppermute | solution.py:266
  31.9 7.0 %collective-permute-done.6.refs_5_ = bf16[2,128,768]{2,1,0:T(8,128)(2,1)S(1)} collective-permute-done((bf16[2,128,768]{2,1,0:T(8,128)(2,1)S(1)}, bf16[2,128,768]{2,1,0:T(8,128)(2,1)S(1)}, u32[]{:S(2)}, u32[]{:S(2)}) %collective-permute-start.6) | collective-permute-done | bytes 393248 | tf_op jit(solution)/shard_map/ppermute | solution.py:266
  38.9 6.5 %shard_map.95 = (bf16[256,1536]{1,0:T(8,128)(2,1)S(1)}, bf16[256,1536]{1,0:T(8,128)(2,1)S(1)}, f32[2,256,768]{2,1,0:T(8,128)S(1)}, bf16[2,128,768]{2,1,0:T(8,128...) custom-call(s32[1,2,4]{2,1,0:T(2,128)S(1)} %bitcast.1, ...), custom_call_target="tpu_custom_call" | custom-call | flops 2113929216 | bytes 7864320 | tf_op jit(solution)/shard_map/pallas_call | solution.py:183
  45.4 0.1 collective-permute-start.11
  45.5 3.2 %collective-permute-start.13 = (bf16[2,128,768]{2,1,0:T(8,128)(2,1)S(1)}, bf16[2,128,768]{2,1,0:T(8,128)(2,1)S(1)}, u32[]{:S(2)}, u32[]{:S(2)}) collective-permute-start(bf16[2,128,768]{2,1,0:T(8,128)(2,1)S(1)} %get-tuple-element.64), channel_id=1, source_target_pairs={{0,8},{1,9},{2,10},{3,11},{4,12},{5,13},{6,14},{7,15},{8,0},{9,1},... | collective-permute-start | bytes 1179656 | tf_op jit(solution)/shard_map/ppermute | solution.py:266
  48.7 2.3 %collective-permute-done.3.refs_5_ = bf16[2,128,768]{2,1,0:T(8,128)(2,1)S(1)} collective-permute-done((bf16[2,128,768]{2,1,0:T(8,128)(2,1)S(1)}, bf16[2,128,768]{2,1,0:T(8,128)(2,1)S(1)}, u32[]{:S(2)}, u32[]{:S(2)}) %collective-permute-start.3) | collective-permute-done | bytes 393248 | tf_op jit(solution)/shard_map/ppermute | solution.py:266
  51.0 6.5 %shard_map.96 = (bf16[256,1536]{1,0:T(8,128)(2,1)S(1)}, bf16[256,1536]{1,0:T(8,128)(2,1)S(1)}, f32[2,256,768]{2,1,0:T(8,128)S(1)}, bf16[2,128,768]{2,1,0:T(8,128...) custom-call(s32[1,2,4]{2,1,0:T(2,128)S(1)} %bitcast.2, ...), custom_call_target="tpu_custom_call", output_to_operand_aliasing={{0}: (10, {}), {1}: (11, {})} | custom-call | flops 2113929216 | bytes 7864320 | tf_op jit(solution)/shard_map/pallas_call | solution.py:183
  57.6 0.1 collective-permute-start.12
  57.6 0.7 collective-permute-start.17
  58.3 8.3 %collective-permute-done.13.refs_0_ = bf16[2,128,768]{2,1,0:T(8,128)(2,1)S(1)} collective-permute-done((bf16[2,128,768]{2,1,0:T(8,128)(2,1)S(1)}, bf16[2,128,768]{2,1,0:T(8,128)(2,1)S(1)}, u32[]{:S(2)}, u32[]{:S(2)}) %collective-permute-start.13) | collective-permute-done | bytes 393248 | tf_op jit(solution)/shard_map/ppermute | solution.py:266
  66.6 1.6 %collective-permute-done.14.refs_1_ = bf16[2,128,768]{2,1,0:T(8,128)(2,1)S(1)} collective-permute-done((bf16[2,128,768]{2,1,0:T(8,128)(2,1)S(1)}, bf16[2,128,768]{2,1,0:T(8,128)(2,1)S(1)}, u32[]{:S(2)}, u32[]{:S(2)}) %collective-permute-start.14) | collective-permute-done | bytes 393248 | tf_op jit(solution)/shard_map/ppermute | solution.py:266
  68.2 0.4 collective-permute-start.9
  68.7 2.5 %collective-permute-start.10 = (bf16[2,128,768]{2,1,0:T(8,128)(2,1)S(1)}, bf16[2,128,768]{2,1,0:T(8,128)(2,1)S(1)}, u32[]{:S(2)}, u32[]{:S(2)}) collective-permute-start(bf16[2,128,768]{2,1,0:T(8,128)(2,1)S(1)} %get-tuple-element.59), channel_id=1, source_target_pairs={{0,2},{1,3},{2,0},{3,1},{4,6},{5,7},{6,4},{7,5},{8,10},{9,11},{10,... | collective-permute-start | bytes 1179656 | tf_op jit(solution)/shard_map/ppermute | solution.py:266
  71.1 0.7 collective-permute-start.16
  71.8 0.9 copy.18
  72.7 0.9 copy.19
  73.6 1.9 %shard_map.97 = (bf16[256,1536]{1,0:T(8,128)(2,1)}, bf16[256,1536]{1,0:T(8,128)(2,1)}) custom-call(s32[1,4]{1,0:T(1,128)S(1)} %copy-done.3, f32[2,256,768]{2,1,0:T(8,128)S(1)} %get-tuple-element.68.own_ref, bf16[2,128,768]{2,1,0:T(8,128)(2,1)S(1)} %collective-permute-done.13.refs_0_, bf16[2,128,768]{2,1,0:T(8,128)(2,1)S(1)} %collective-permute-done.14.refs_1_, ...), custom_call_target="tpu_custom_call" | custom-call | bytes 3145728 | tf_op jit(solution)/shard_map/pallas_call | solution.py:234
  75.4 10.3 %collective-permute-done.8.refs_0_ = bf16[2,128,768]{2,1,0:T(8,128)(2,1)S(1)} collective-permute-done((bf16[2,128,768]{2,1,0:T(8,128)(2,1)S(1)}, bf16[2,128,768]{2,1,0:T(8,128)(2,1)S(1)}, u32[]{:S(2)}, u32[]{:S(2)}) %collective-permute-start.8) | collective-permute-done | bytes 393248 | tf_op jit(solution)/shard_map/ppermute | solution.py:266
  85.7 1.5 %collective-permute-done.9.refs_1_ = bf16[2,128,768]{2,1,0:T(8,128)(2,1)S(1)} collective-permute-done((bf16[2,128,768]{2,1,0:T(8,128)(2,1)S(1)}, bf16[2,128,768]{2,1,0:T(8,128)(2,1)S(1)}, u32[]{:S(2)}, u32[]{:S(2)}) %collective-permute-start.9) | collective-permute-done | bytes 393248 | tf_op jit(solution)/shard_map/ppermute | solution.py:266
  87.2 1.9 %shard_map.98 = (bf16[256,1536]{1,0:T(8,128)(2,1)}, bf16[256,1536]{1,0:T(8,128)(2,1)}) custom-call(s32[1,4]{1,0:T(1,128)S(1)} %copy-done.3, f32[2,256,768]{2,1,0:T(8,128)S(1)} %get-tuple-element.56.own_ref, bf16[2,128,768]{2,1,0:T(8,128)(2,1)S(1)} %collective-permute-done.8.refs_0_, ...), custom_call_target="tpu_custom_call", output_to_operand_aliasing={{0}: (7, {}), {1}: (8, {})} | custom-call | bytes 3145728 | tf_op jit(solution)/shard_map/pallas_call | solution.py:234
  (26 shorter events, 0.1 us)
Async XLA Ops:
  0.6 38.3 %copy-start.1 = (bf16[256,1536]{1,0:T(8,128)(2,1)S(1)}, bf16[256,1536]{1,0:T(8,128)(2,1)}, u32[]{:S(2)}) copy-start(bf16[256,1536]{1,0:T(8,128)(2,1)} %refs_3_.3) | copy-start | bytes 2359300
  0.6 38.3 %copy-start = (bf16[256,1536]{1,0:T(8,128)(2,1)S(1)}, bf16[256,1536]{1,0:T(8,128)(2,1)}, u32[]{:S(2)}) copy-start(bf16[256,1536]{1,0:T(8,128)(2,1)} %refs_2_.3) | copy-start | bytes 2359300
  0.7 0.8 copy-start.2
  1.4 12.0 %copy-start.3 = (s32[1,4]{1,0:T(1,128)S(1)}, s32[1,4]{1,0:T(1,128)}, u32[]{:S(2)}) copy-start(s32[1,4]{1,0:T(1,128)} %pick_ref.7) | copy-start | bytes 52
  1.4 37.5 %copy-start.4 = (bf16[256,1536]{1,0:T(8,128)(2,1)S(1)}, bf16[256,1536]{1,0:T(8,128)(2,1)}, u32[]{:S(2)}) copy-start(bf16[256,1536]{1,0:T(8,128)(2,1)} %refs_0_.3) | copy-start | bytes 2359300
  1.4 37.5 %copy-start.5 = (bf16[256,1536]{1,0:T(8,128)(2,1)S(1)}, bf16[256,1536]{1,0:T(8,128)(2,1)}, u32[]{:S(2)}) copy-start(bf16[256,1536]{1,0:T(8,128)(2,1)} %refs_1_.3) | copy-start | bytes 2359300
  1.4 37.5 %copy-start.6 = (s32[1,4,2]{1,2,0:T(2,128)S(1)}, s32[1,4,2]{1,2,0:T(2,128)}, u32[]{:S(2)}) copy-start(s32[1,4,2]{1,2,0:T(2,128)} %param.10) | copy-start | bytes 100
  4.0 22.3 %collective-permute-start.1 = (bf16[2,192,1536]{2,1,0:T(8,128)(2,1)S(1)}, bf16[2,192,1536]{2,1,0:T(8,128)(2,1)S(1)}, u32[]{:S(2)}, u32[]{:S(2)}) collective-permute-start(bf16[2,192,1536]{2,1,0:T(8,128)(2,1)S(1)} %get-tuple-element.43), channel_id=1, source_target_pairs={{0,1},{1,0},{2,3},{3,2},{4,5},{5,4},{6,7},{7,6},{8,9},{9,8},{10,11... | collective-permute-start | bytes 3538952 | tf_op jit(solution)/shard_map/ppermute | solution.py:266
  4.6 21.7 %collective-permute-start = (bf16[2,128,768]{2,1,0:T(8,128)(2,1)S(1)}, bf16[2,128,768]{2,1,0:T(8,128)(2,1)S(1)}, u32[]{:S(2)}, u32[]{:S(2)}) collective-permute-start(bf16[2,128,768]{2,1,0:T(8,128)(2,1)S(1)} %get-tuple-element.39), channel_id=1, source_target_pairs={{0,8},{1,9},{2,10},{3,11},{4,12},{5,13},{6,14},{7,15},{8,0},{9,1},... | collective-permute-start | bytes 1179656 | tf_op jit(solution)/shard_map/ppermute | solution.py:266
  8.2 22.2 %collective-permute-start.5 = (bf16[2,64,1536]{2,1,0:T(8,128)(2,1)S(1)}, bf16[2,64,1536]{2,1,0:T(8,128)(2,1)S(1)}, u32[]{:S(2)}, u32[]{:S(2)}) collective-permute-start(bf16[2,64,1536]{2,1,0:T(8,128)(2,1)S(1)} %get-tuple-element.49), channel_id=1, source_target_pairs={{0,0},{1,2},{2,1},{3,4},{4,3},{5,6},{6,5},{7,8},{8,7},{9,10},{10,9... | collective-permute-start | bytes 1179656 | tf_op jit(solution)/shard_map/ppermute | solution.py:266
  8.9 30.0 %collective-permute-start.6 = (bf16[2,128,768]{2,1,0:T(8,128)(2,1)S(1)}, bf16[2,128,768]{2,1,0:T(8,128)(2,1)S(1)}, u32[]{:S(2)}, u32[]{:S(2)}) collective-permute-start(bf16[2,128,768]{2,1,0:T(8,128)(2,1)S(1)} %get-tuple-element.50), channel_id=1, source_target_pairs={{0,4},{1,5},{2,6},{3,7},{4,0},{5,1},{6,2},{7,3},{8,12},{9,13},{10,... | collective-permute-start | bytes 1179656 | tf_op jit(solution)/shard_map/ppermute | solution.py:266
  12.8 26.1 %collective-permute-start.7 = (bf16[2,128,768]{2,1,0:T(8,128)(2,1)S(1)}, bf16[2,128,768]{2,1,0:T(8,128)(2,1)S(1)}, u32[]{:S(2)}, u32[]{:S(2)}) collective-permute-start(bf16[2,128,768]{2,1,0:T(8,128)(2,1)S(1)} %get-tuple-element.51), channel_id=1, source_target_pairs={{0,2},{1,3},{2,0},{3,1},{4,6},{5,7},{6,4},{7,5},{8,10},{9,11},{10,... | collective-permute-start | bytes 1179656 | tf_op jit(solution)/shard_map/ppermute | solution.py:266
  26.3 22.4 %collective-permute-start.2 = (bf16[2,128,768]{2,1,0:T(8,128)(2,1)S(1)}, bf16[2,128,768]{2,1,0:T(8,128)(2,1)S(1)}, u32[]{:S(2)}, u32[]{:S(2)}) collective-permute-start(bf16[2,128,768]{2,1,0:T(8,128)(2,1)S(1)} %get-tuple-element.44), channel_id=1, source_target_pairs={{0,8},{1,9},{2,10},{3,11},{4,12},{5,13},{6,14},{7,15},{8,0},{9,1},... | collective-permute-start | bytes 1179656 | tf_op jit(solution)/shard_map/ppermute | solution.py:266
  26.3 24.7 %collective-permute-start.3 = (bf16[2,128,768]{2,1,0:T(8,128)(2,1)S(1)}, bf16[2,128,768]{2,1,0:T(8,128)(2,1)S(1)}, u32[]{:S(2)}, u32[]{:S(2)}) collective-permute-start(bf16[2,128,768]{2,1,0:T(8,128)(2,1)S(1)} %get-tuple-element.46), channel_id=1, source_target_pairs={{0,4},{1,5},{2,6},{3,7},{4,0},{5,1},{6,2},{7,3},{8,12},{9,13},{10,... | collective-permute-start | bytes 1179656 | tf_op jit(solution)/shard_map/ppermute | solution.py:266
  30.4 20.6 %collective-permute-start.4 = (bf16[2,128,768]{2,1,0:T(8,128)(2,1)S(1)}, bf16[2,128,768]{2,1,0:T(8,128)(2,1)S(1)}, u32[]{:S(2)}, u32[]{:S(2)}) collective-permute-start(bf16[2,128,768]{2,1,0:T(8,128)(2,1)S(1)} %get-tuple-element.48), channel_id=1, source_target_pairs={{0,2},{1,3},{2,0},{3,1},{4,6},{5,7},{6,4},{7,5},{8,10},{9,11},{10,... | collective-permute-start | bytes 1179656 | tf_op jit(solution)/shard_map/ppermute | solution.py:266
  45.4 12.1 %collective-permute-start.11 = (bf16[2,192,768]{2,1,0:T(8,128)(2,1)S(1)}, bf16[2,192,768]{2,1,0:T(8,128)(2,1)S(1)}, u32[]{:S(2)}, u32[]{:S(2)}) collective-permute-start(bf16[2,192,768]{2,1,0:T(8,128)(2,1)S(1)} %get-tuple-element.61), channel_id=1, source_target_pairs={{0,1},{1,0},{2,3},{3,2},{4,5},{5,4},{6,7},{7,6},{8,9},{9,8},{10,11... | collective-permute-start | bytes 1769480 | tf_op jit(solution)/shard_map/ppermute | solution.py:266
  45.5 21.1 %collective-permute-start.13 = (bf16[2,128,768]{2,1,0:T(8,128)(2,1)S(1)}, bf16[2,128,768]{2,1,0:T(8,128)(2,1)S(1)}, u32[]{:S(2)}, u32[]{:S(2)}) collective-permute-start(bf16[2,128,768]{2,1,0:T(8,128)(2,1)S(1)} %get-tuple-element.64), channel_id=1, source_target_pairs={{0,8},{1,9},{2,10},{3,11},{4,12},{5,13},{6,14},{7,15},{8,0},{9,1},... | collective-permute-start | bytes 1179656 | tf_op jit(solution)/shard_map/ppermute | solution.py:266
  48.7 19.5 %collective-permute-start.14 = (bf16[2,128,768]{2,1,0:T(8,128)(2,1)S(1)}, bf16[2,128,768]{2,1,0:T(8,128)(2,1)S(1)}, u32[]{:S(2)}, u32[]{:S(2)}) collective-permute-start(bf16[2,128,768]{2,1,0:T(8,128)(2,1)S(1)} %get-tuple-element.65), channel_id=1, source_target_pairs={{0,4},{1,5},{2,6},{3,7},{4,0},{5,1},{6,2},{7,3},{8,12},{9,13},{10,... | collective-permute-start | bytes 1179656 | tf_op jit(solution)/shard_map/ppermute | solution.py:266
  51.0 17.6 %collective-permute-start.15 = (bf16[2,128,768]{2,1,0:T(8,128)(2,1)S(1)}, bf16[2,128,768]{2,1,0:T(8,128)(2,1)S(1)}, u32[]{:S(2)}, u32[]{:S(2)}) collective-permute-start(bf16[2,128,768]{2,1,0:T(8,128)(2,1)S(1)} %get-tuple-element.66), channel_id=1, source_target_pairs={{0,2},{1,3},{2,0},{3,1},{4,6},{5,7},{6,4},{7,5},{8,10},{9,11},{10,... | collective-permute-start | bytes 1179656 | tf_op jit(solution)/shard_map/ppermute | solution.py:266
  57.6 29.6 %collective-permute-start.12 = (bf16[2,192,768]{2,1,0:T(8,128)(2,1)S(1)}, bf16[2,192,768]{2,1,0:T(8,128)(2,1)S(1)}, u32[]{:S(2)}, u32[]{:S(2)}) collective-permute-start(bf16[2,192,768]{2,1,0:T(8,128)(2,1)S(1)} %get-tuple-element.62), channel_id=1, source_target_pairs={{0,1},{1,0},{2,3},{3,2},{4,5},{5,4},{6,7},{7,6},{8,9},{9,8},{10,11... | collective-permute-start | bytes 1769480 | tf_op jit(solution)/shard_map/ppermute | solution.py:266
  57.6 13.5 %collective-permute-start.17 = (bf16[2,64,768]{2,1,0:T(8,128)(2,1)S(1)}, bf16[2,64,768]{2,1,0:T(8,128)(2,1)S(1)}, u32[]{:S(2)}, u32[]{:S(2)}) collective-permute-start(bf16[2,64,768]{2,1,0:T(8,128)(2,1)S(1)} %get-tuple-element.69), channel_id=1, source_target_pairs={{0,0},{1,2},{2,1},{3,4},{4,3},{5,6},{6,5},{7,8},{8,7},{9,10},{10,9... | collective-permute-start | bytes 589832 | tf_op jit(solution)/shard_map/ppermute | solution.py:266
  66.6 19.1 %collective-permute-start.8 = (bf16[2,128,768]{2,1,0:T(8,128)(2,1)S(1)}, bf16[2,128,768]{2,1,0:T(8,128)(2,1)S(1)}, u32[]{:S(2)}, u32[]{:S(2)}) collective-permute-start(bf16[2,128,768]{2,1,0:T(8,128)(2,1)S(1)} %get-tuple-element.57), channel_id=1, source_target_pairs={{0,8},{1,9},{2,10},{3,11},{4,12},{5,13},{6,14},{7,15},{8,0},{9,1},... | collective-permute-start | bytes 1179656 | tf_op jit(solution)/shard_map/ppermute | solution.py:266
  68.2 19.0 %collective-permute-start.9 = (bf16[2,128,768]{2,1,0:T(8,128)(2,1)S(1)}, bf16[2,128,768]{2,1,0:T(8,128)(2,1)S(1)}, u32[]{:S(2)}, u32[]{:S(2)}) collective-permute-start(bf16[2,128,768]{2,1,0:T(8,128)(2,1)S(1)} %get-tuple-element.58), channel_id=1, source_target_pairs={{0,4},{1,5},{2,6},{3,7},{4,0},{5,1},{6,2},{7,3},{8,12},{9,13},{10,... | collective-permute-start | bytes 1179656 | tf_op jit(solution)/shard_map/ppermute | solution.py:266
  68.7 18.5 %collective-permute-start.10 = (bf16[2,128,768]{2,1,0:T(8,128)(2,1)S(1)}, bf16[2,128,768]{2,1,0:T(8,128)(2,1)S(1)}, u32[]{:S(2)}, u32[]{:S(2)}) collective-permute-start(bf16[2,128,768]{2,1,0:T(8,128)(2,1)S(1)} %get-tuple-element.59), channel_id=1, source_target_pairs={{0,2},{1,3},{2,0},{3,1},{4,6},{5,7},{6,4},{7,5},{8,10},{9,11},{10,... | collective-permute-start | bytes 1179656 | tf_op jit(solution)/shard_map/ppermute | solution.py:266
  71.1 4.3 %collective-permute-start.16 = (bf16[2,64,768]{2,1,0:T(8,128)(2,1)S(1)}, bf16[2,64,768]{2,1,0:T(8,128)(2,1)S(1)}, u32[]{:S(2)}, u32[]{:S(2)}) collective-permute-start(bf16[2,64,768]{2,1,0:T(8,128)(2,1)S(1)} %get-tuple-element.67), channel_id=1, source_target_pairs={{0,0},{1,2},{2,1},{3,4},{4,3},{5,6},{6,5},{7,8},{8,7},{9,10},{10,9... | collective-permute-start | bytes 589832 | tf_op jit(solution)/shard_map/ppermute | solution.py:266

commit v2 on v1

--- a/solution.py
+++ b/solution.py
@@ -206,17 +206,22 @@
     tokens = own_ref.shape[1]
     starts = [[start_of(kind, pick_ref, tokens) for kind, _ in parts] for parts in rows]
     copies = []
-    for side in range(2):
-        acc[...] = own_ref[side]
+    step = heads * HDIM // 2
+    for side, at_col in ((side, col) for side in range(2) for col in (0, step)):
+        cols = pl.ds(at_col, step)
+        acc[:, cols] = own_ref[side, :, cols]
         for ref, parts, spots in zip(got, rows, starts, strict=True):
             at = 0
-            cut = slice(None) if ref.shape[2] == heads * HDIM else slice(head * HDIM, (head + heads) * HDIM)
+            whole = ref.shape[2] != heads * HDIM
+            cut = pl.ds(at_col + (head * HDIM if whole else 0), step)
             for (_, size), start in zip(parts, spots, strict=True):
-                acc[pl.ds(start, size)] += ref[side, at : at + size, cut].astype(F32)
+                acc[pl.ds(start, size), cols] += ref[side, at : at + size, cut].astype(F32)
                 at += size
-        done[side] = acc[...].astype(BF16)
-        target = outs[side].at[:, pl.ds(head * HDIM, heads * HDIM)]
-        copies.append(pltpu.make_async_copy(done.at[side], target, sem.at[side]))
+        done[side, :, cols] = acc[:, cols].astype(BF16)
+        target = outs[side].at[:, pl.ds(head * HDIM + at_col, step)]
+        copies.append(
+            pltpu.make_async_copy(done.at[side, :, cols], target, sem.at[len(copies)])
+        )
         copies[-1].start()
     for copy in copies:
         copy.wait()
@@ -239,7 +244,7 @@
         scratch_shapes=[
             pltpu.VMEM((tokens, heads * HDIM), F32),
             pltpu.VMEM((2, tokens, heads * HDIM), BF16),
-            pltpu.SemaphoreType.DMA((2,)),
+            pltpu.SemaphoreType.DMA((4,)),
         ],
         input_output_aliases=aliases,
         compiler_params=pltpu.CompilerParams(vmem_limit_bytes=8 << 20),

time: 90.4 us -> 90.4 us (level)
  no operation moved by 1% of the time
where the time goes in v2:
time: 90.4 us; the launch traced here: 89 us
  waiting for transfers between devices  41.7 us (46%)
  starting transfers between devices  22.7 us (25%)
  Pallas kernels  21.2 us (23%)
  local copies, waits for them, and re-layouts  2.55 us (3%)
    ppermute x18, waiting for transfers between devices, send(): lax.ppermute(piece, 'frame', t)  41.7 us
    ppermute x18, starting transfers between devices, send(): lax.ppermute(piece, 'frame', t)  22.7 us
    pallas_call x2, Pallas kernels, attend(): pl.pallas_call(functools.partial(attend_kernel, head, heads, rows, len(al...  13 us
    pallas_call x2, Pallas kernels, pack(): pl.pallas_call(functools.partial(pack_kernel, pieces), out_shape=[pltpu.V...  4.55 us
    pallas_call x2, Pallas kernels, combine(): pl.pallas_call(functools.partial(combine_kernel, head, heads, rows, len(a...  3.66 us
    unnamed x16, local copies, waits for them, and re-layouts  2.55 us
  transfers between devices with their start and end apart: 18, of which 7 were waited for; matrix products, arithmetic and copies ran while one was open for 2% of the time, Pallas kernels for 19%

profile of v2, /device:TPU:0, one launch (start us, length us, event | category | flops | bytes accessed | tf_op | source)
XLA Modules:
  0.0 89.0 jit_solution(2191110777437604482)
XLA Ops:
  0.6 0.0 copy-start.1
  0.6 0.0 copy-start
  0.7 0.8 copy-done.2
  1.4 2.6 %shard_map.93 = (bf16[2,192,1536]{2,1,0:T(8,128)(2,1)S(1)}, bf16[2,64,1536]{2,1,0:T(8,128)(2,1)S(1)}, bf16[2,128,768]{2,1,0:T(8,128)(2,1)S(1)}, bf16[2,128,768]{2,1,0:T(8,128)(2,1)S(1)}, bf16[2,128,768]{2,1,0:T(8,128)(2,1)S(1)}) custom-call(s32[1,4]{1,0:T(1,128)S(1)} %copy-done.2, bf16[256,1536]{1,0:T(8,128)(2,1)} %refs_2_.3, bf16[256,1536]{1,0:T(8,128)(2,1)} %refs_3_.3), custom_call_target="tpu_custom_call" | custom-call | bytes 5505024 | tf_op jit(solution)/shard_map/pallas_call | solution.py:76
  4.0 0.4 collective-permute-start.1
  4.4 3.8 %collective-permute-start = (bf16[2,128,768]{2,1,0:T(8,128)(2,1)S(1)}, bf16[2,128,768]{2,1,0:T(8,128)(2,1)S(1)}, u32[]{:S(2)}, u32[]{:S(2)}) collective-permute-start(bf16[2,128,768]{2,1,0:T(8,128)(2,1)S(1)} %get-tuple-element.39), channel_id=1, source_target_pairs={{0,8},{1,9},{2,10},{3,11},{4,12},{5,13},{6,14},{7,15},{8,0},{9,1},... | collective-permute-start | bytes 1179656 | tf_op jit(solution)/shard_map/ppermute | solution.py:271
  8.2 0.7 collective-permute-start.5
  8.9 3.9 %collective-permute-start.6 = (bf16[2,128,768]{2,1,0:T(8,128)(2,1)S(1)}, bf16[2,128,768]{2,1,0:T(8,128)(2,1)S(1)}, u32[]{:S(2)}, u32[]{:S(2)}) collective-permute-start(bf16[2,128,768]{2,1,0:T(8,128)(2,1)S(1)} %get-tuple-element.50), channel_id=1, source_target_pairs={{0,4},{1,5},{2,6},{3,7},{4,0},{5,1},{6,2},{7,3},{8,12},{9,13},{10,... | collective-permute-start | bytes 1179656 | tf_op jit(solution)/shard_map/ppermute | solution.py:271
  12.8 0.8 collective-permute-start.7
  13.6 2.0 %shard_map.94 = (bf16[2,128,768]{2,1,0:T(8,128)(2,1)S(1)}, bf16[2,128,768]{2,1,0:T(8,128)(2,1)S(1)}, bf16[2,128,768]{2,1,0:T(8,128)(2,1)S(1)}) custom-call(s32[1,4]{1,0:T(1,128)S(1)} %copy-done.3, bf16[256,1536]{1,0:T(8,128)(2,1)} %refs_2_.3, bf16[256,1536]{1,0:T(8,128)(2,1)} %refs_3_.3), custom_call_target="tpu_custom_call" | custom-call | bytes 2359296 | tf_op jit(solution)/shard_map/pallas_call | solution.py:76
  15.5 10.9 %collective-permute-done.refs_4_ = bf16[2,128,768]{2,1,0:T(8,128)(2,1)S(1)} collective-permute-done((bf16[2,128,768]{2,1,0:T(8,128)(2,1)S(1)}, bf16[2,128,768]{2,1,0:T(8,128)(2,1)S(1)}, u32[]{:S(2)}, u32[]{:S(2)}) %collective-permute-start) | collective-permute-done | bytes 393248 | tf_op jit(solution)/shard_map/ppermute | solution.py:271
  26.5 4.1 %collective-permute-start.3 = (bf16[2,128,768]{2,1,0:T(8,128)(2,1)S(1)}, bf16[2,128,768]{2,1,0:T(8,128)(2,1)S(1)}, u32[]{:S(2)}, u32[]{:S(2)}) collective-permute-start(bf16[2,128,768]{2,1,0:T(8,128)(2,1)S(1)} %get-tuple-element.46), channel_id=1, source_target_pairs={{0,4},{1,5},{2,6},{3,7},{4,0},{5,1},{6,2},{7,3},{8,12},{9,13},{10,... | collective-permute-start | bytes 1179656 | tf_op jit(solution)/shard_map/ppermute | solution.py:271
  30.6 1.4 %collective-permute-start.4 = (bf16[2,128,768]{2,1,0:T(8,128)(2,1)S(1)}, bf16[2,128,768]{2,1,0:T(8,128)(2,1)S(1)}, u32[]{:S(2)}, u32[]{:S(2)}) collective-permute-start(bf16[2,128,768]{2,1,0:T(8,128)(2,1)S(1)} %get-tuple-element.48), channel_id=1, source_target_pairs={{0,2},{1,3},{2,0},{3,1},{4,6},{5,7},{6,4},{7,5},{8,10},{9,11},{10,... | collective-permute-start | bytes 1179656 | tf_op jit(solution)/shard_map/ppermute | solution.py:271
  31.9 6.8 %collective-permute-done.6.refs_5_ = bf16[2,128,768]{2,1,0:T(8,128)(2,1)S(1)} collective-permute-done((bf16[2,128,768]{2,1,0:T(8,128)(2,1)S(1)}, bf16[2,128,768]{2,1,0:T(8,128)(2,1)S(1)}, u32[]{:S(2)}, u32[]{:S(2)}) %collective-permute-start.6) | collective-permute-done | bytes 393248 | tf_op jit(solution)/shard_map/ppermute | solution.py:271
  38.7 6.5 %shard_map.95 = (bf16[256,1536]{1,0:T(8,128)(2,1)S(1)}, bf16[256,1536]{1,0:T(8,128)(2,1)S(1)}, f32[2,256,768]{2,1,0:T(8,128)S(1)}, bf16[2,128,768]{2,1,0:T(8,128...) custom-call(s32[1,2,4]{2,1,0:T(2,128)S(1)} %bitcast.1, ...), custom_call_target="tpu_custom_call" | custom-call | flops 2113929216 | bytes 7864320 | tf_op jit(solution)/shard_map/pallas_call | solution.py:183
  45.3 0.1 collective-permute-start.11
  45.3 3.4 %collective-permute-start.13 = (bf16[2,128,768]{2,1,0:T(8,128)(2,1)S(1)}, bf16[2,128,768]{2,1,0:T(8,128)(2,1)S(1)}, u32[]{:S(2)}, u32[]{:S(2)}) collective-permute-start(bf16[2,128,768]{2,1,0:T(8,128)(2,1)S(1)} %get-tuple-element.64), channel_id=1, source_target_pairs={{0,8},{1,9},{2,10},{3,11},{4,12},{5,13},{6,14},{7,15},{8,0},{9,1},... | collective-permute-start | bytes 1179656 | tf_op jit(solution)/shard_map/ppermute | solution.py:271
  48.7 2.3 %collective-permute-done.3.refs_5_ = bf16[2,128,768]{2,1,0:T(8,128)(2,1)S(1)} collective-permute-done((bf16[2,128,768]{2,1,0:T(8,128)(2,1)S(1)}, bf16[2,128,768]{2,1,0:T(8,128)(2,1)S(1)}, u32[]{:S(2)}, u32[]{:S(2)}) %collective-permute-start.3) | collective-permute-done | bytes 393248 | tf_op jit(solution)/shard_map/ppermute | solution.py:271
  51.0 6.5 %shard_map.96 = (bf16[256,1536]{1,0:T(8,128)(2,1)S(1)}, bf16[256,1536]{1,0:T(8,128)(2,1)S(1)}, f32[2,256,768]{2,1,0:T(8,128)S(1)}, bf16[2,128,768]{2,1,0:T(8,128...) custom-call(s32[1,2,4]{2,1,0:T(2,128)S(1)} %bitcast.2, ...), custom_call_target="tpu_custom_call", output_to_operand_aliasing={{0}: (10, {}), {1}: (11, {})} | custom-call | flops 2113929216 | bytes 7864320 | tf_op jit(solution)/shard_map/pallas_call | solution.py:183
  57.5 0.1 collective-permute-start.12
  57.6 0.7 collective-permute-start.17
  58.3 8.3 %collective-permute-done.13.refs_0_ = bf16[2,128,768]{2,1,0:T(8,128)(2,1)S(1)} collective-permute-done((bf16[2,128,768]{2,1,0:T(8,128)(2,1)S(1)}, bf16[2,128,768]{2,1,0:T(8,128)(2,1)S(1)}, u32[]{:S(2)}, u32[]{:S(2)}) %collective-permute-start.13) | collective-permute-done | bytes 393248 | tf_op jit(solution)/shard_map/ppermute | solution.py:271
  66.6 1.6 %collective-permute-done.14.refs_1_ = bf16[2,128,768]{2,1,0:T(8,128)(2,1)S(1)} collective-permute-done((bf16[2,128,768]{2,1,0:T(8,128)(2,1)S(1)}, bf16[2,128,768]{2,1,0:T(8,128)(2,1)S(1)}, u32[]{:S(2)}, u32[]{:S(2)}) %collective-permute-start.14) | collective-permute-done | bytes 393248 | tf_op jit(solution)/shard_map/ppermute | solution.py:271
  68.2 0.4 collective-permute-start.9
  68.7 2.5 %collective-permute-start.10 = (bf16[2,128,768]{2,1,0:T(8,128)(2,1)S(1)}, bf16[2,128,768]{2,1,0:T(8,128)(2,1)S(1)}, u32[]{:S(2)}, u32[]{:S(2)}) collective-permute-start(bf16[2,128,768]{2,1,0:T(8,128)(2,1)S(1)} %get-tuple-element.59), channel_id=1, source_target_pairs={{0,2},{1,3},{2,0},{3,1},{4,6},{5,7},{6,4},{7,5},{8,10},{9,11},{10,... | collective-permute-start | bytes 1179656 | tf_op jit(solution)/shard_map/ppermute | solution.py:271
  71.1 0.7 collective-permute-start.16
  71.8 0.9 copy.18
  72.7 0.9 copy.19
  73.6 1.8 %shard_map.97 = (bf16[256,1536]{1,0:T(8,128)(2,1)}, bf16[256,1536]{1,0:T(8,128)(2,1)}) custom-call(s32[1,4]{1,0:T(1,128)S(1)} %copy-done.3, f32[2,256,768]{2,1,0:T(8,128)S(1)} %get-tuple-element.68.own_ref, bf16[2,128,768]{2,1,0:T(8,128)(2,1)S(1)} %collective-permute-done.13.refs_0_, bf16[2,128,768]{2,1,0:T(8,128)(2,1)S(1)} %collective-permute-done.14.refs_1_, ...), custom_call_target="tpu_custom_call" | custom-call | bytes 3145728 | tf_op jit(solution)/shard_map/pallas_call | solution.py:239
  75.4 10.5 %collective-permute-done.8.refs_0_ = bf16[2,128,768]{2,1,0:T(8,128)(2,1)S(1)} collective-permute-done((bf16[2,128,768]{2,1,0:T(8,128)(2,1)S(1)}, bf16[2,128,768]{2,1,0:T(8,128)(2,1)S(1)}, u32[]{:S(2)}, u32[]{:S(2)}) %collective-permute-start.8) | collective-permute-done | bytes 393248 | tf_op jit(solution)/shard_map/ppermute | solution.py:271
  85.9 1.3 %collective-permute-done.9.refs_1_ = bf16[2,128,768]{2,1,0:T(8,128)(2,1)S(1)} collective-permute-done((bf16[2,128,768]{2,1,0:T(8,128)(2,1)S(1)}, bf16[2,128,768]{2,1,0:T(8,128)(2,1)S(1)}, u32[]{:S(2)}, u32[]{:S(2)}) %collective-permute-start.9) | collective-permute-done | bytes 393248 | tf_op jit(solution)/shard_map/ppermute | solution.py:271
  87.2 1.8 %shard_map.98 = (bf16[256,1536]{1,0:T(8,128)(2,1)}, bf16[256,1536]{1,0:T(8,128)(2,1)}) custom-call(s32[1,4]{1,0:T(1,128)S(1)} %copy-done.3, f32[2,256,768]{2,1,0:T(8,128)S(1)} %get-tuple-element.56.own_ref, bf16[2,128,768]{2,1,0:T(8,128)(2,1)S(1)} %collective-permute-done.8.refs_0_, ...), custom_call_target="tpu_custom_call", output_to_operand_aliasing={{0}: (7, {}), {1}: (8, {})} | custom-call | bytes 3145728 | tf_op jit(solution)/shard_map/pallas_call | solution.py:239
  (26 shorter events, 0.1 us)
Async XLA Ops:
  0.6 38.1 %copy-start.1 = (bf16[256,1536]{1,0:T(8,128)(2,1)S(1)}, bf16[256,1536]{1,0:T(8,128)(2,1)}, u32[]{:S(2)}) copy-start(bf16[256,1536]{1,0:T(8,128)(2,1)} %refs_3_.3) | copy-start | bytes 2359300
  0.6 38.1 %copy-start = (bf16[256,1536]{1,0:T(8,128)(2,1)S(1)}, bf16[256,1536]{1,0:T(8,128)(2,1)}, u32[]{:S(2)}) copy-start(bf16[256,1536]{1,0:T(8,128)(2,1)} %refs_2_.3) | copy-start | bytes 2359300
  0.7 0.8 copy-start.2
  1.4 12.1 %copy-start.3 = (s32[1,4]{1,0:T(1,128)S(1)}, s32[1,4]{1,0:T(1,128)}, u32[]{:S(2)}) copy-start(s32[1,4]{1,0:T(1,128)} %pick_ref.7) | copy-start | bytes 52
  1.4 37.3 %copy-start.4 = (bf16[256,1536]{1,0:T(8,128)(2,1)S(1)}, bf16[256,1536]{1,0:T(8,128)(2,1)}, u32[]{:S(2)}) copy-start(bf16[256,1536]{1,0:T(8,128)(2,1)} %refs_0_.3) | copy-start | bytes 2359300
  1.4 37.3 %copy-start.5 = (bf16[256,1536]{1,0:T(8,128)(2,1)S(1)}, bf16[256,1536]{1,0:T(8,128)(2,1)}, u32[]{:S(2)}) copy-start(bf16[256,1536]{1,0:T(8,128)(2,1)} %refs_1_.3) | copy-start | bytes 2359300
  1.4 37.3 %copy-start.6 = (s32[1,4,2]{1,2,0:T(2,128)S(1)}, s32[1,4,2]{1,2,0:T(2,128)}, u32[]{:S(2)}) copy-start(s32[1,4,2]{1,2,0:T(2,128)} %param.10) | copy-start | bytes 100
  4.0 22.4 %collective-permute-start.1 = (bf16[2,192,1536]{2,1,0:T(8,128)(2,1)S(1)}, bf16[2,192,1536]{2,1,0:T(8,128)(2,1)S(1)}, u32[]{:S(2)}, u32[]{:S(2)}) collective-permute-start(bf16[2,192,1536]{2,1,0:T(8,128)(2,1)S(1)} %get-tuple-element.43), channel_id=1, source_target_pairs={{0,1},{1,0},{2,3},{3,2},{4,5},{5,4},{6,7},{7,6},{8,9},{9,8},{10,11... | collective-permute-start | bytes 3538952 | tf_op jit(solution)/shard_map/ppermute | solution.py:271
  4.4 22.1 %collective-permute-start = (bf16[2,128,768]{2,1,0:T(8,128)(2,1)S(1)}, bf16[2,128,768]{2,1,0:T(8,128)(2,1)S(1)}, u32[]{:S(2)}, u32[]{:S(2)}) collective-permute-start(bf16[2,128,768]{2,1,0:T(8,128)(2,1)S(1)} %get-tuple-element.39), channel_id=1, source_target_pairs={{0,8},{1,9},{2,10},{3,11},{4,12},{5,13},{6,14},{7,15},{8,0},{9,1},... | collective-permute-start | bytes 1179656 | tf_op jit(solution)/shard_map/ppermute | solution.py:271
  8.2 22.4 %collective-permute-start.5 = (bf16[2,64,1536]{2,1,0:T(8,128)(2,1)S(1)}, bf16[2,64,1536]{2,1,0:T(8,128)(2,1)S(1)}, u32[]{:S(2)}, u32[]{:S(2)}) collective-permute-start(bf16[2,64,1536]{2,1,0:T(8,128)(2,1)S(1)} %get-tuple-element.49), channel_id=1, source_target_pairs={{0,0},{1,2},{2,1},{3,4},{4,3},{5,6},{6,5},{7,8},{8,7},{9,10},{10,9... | collective-permute-start | bytes 1179656 | tf_op jit(solution)/shard_map/ppermute | solution.py:271
  8.9 29.8 %collective-permute-start.6 = (bf16[2,128,768]{2,1,0:T(8,128)(2,1)S(1)}, bf16[2,128,768]{2,1,0:T(8,128)(2,1)S(1)}, u32[]{:S(2)}, u32[]{:S(2)}) collective-permute-start(bf16[2,128,768]{2,1,0:T(8,128)(2,1)S(1)} %get-tuple-element.50), channel_id=1, source_target_pairs={{0,4},{1,5},{2,6},{3,7},{4,0},{5,1},{6,2},{7,3},{8,12},{9,13},{10,... | collective-permute-start | bytes 1179656 | tf_op jit(solution)/shard_map/ppermute | solution.py:271
  12.8 25.9 %collective-permute-start.7 = (bf16[2,128,768]{2,1,0:T(8,128)(2,1)S(1)}, bf16[2,128,768]{2,1,0:T(8,128)(2,1)S(1)}, u32[]{:S(2)}, u32[]{:S(2)}) collective-permute-start(bf16[2,128,768]{2,1,0:T(8,128)(2,1)S(1)} %get-tuple-element.51), channel_id=1, source_target_pairs={{0,2},{1,3},{2,0},{3,1},{4,6},{5,7},{6,4},{7,5},{8,10},{9,11},{10,... | collective-permute-start | bytes 1179656 | tf_op jit(solution)/shard_map/ppermute | solution.py:271
  26.5 22.3 %collective-permute-start.2 = (bf16[2,128,768]{2,1,0:T(8,128)(2,1)S(1)}, bf16[2,128,768]{2,1,0:T(8,128)(2,1)S(1)}, u32[]{:S(2)}, u32[]{:S(2)}) collective-permute-start(bf16[2,128,768]{2,1,0:T(8,128)(2,1)S(1)} %get-tuple-element.44), channel_id=1, source_target_pairs={{0,8},{1,9},{2,10},{3,11},{4,12},{5,13},{6,14},{7,15},{8,0},{9,1},... | collective-permute-start | bytes 1179656 | tf_op jit(solution)/shard_map/ppermute | solution.py:271
  26.5 24.5 %collective-permute-start.3 = (bf16[2,128,768]{2,1,0:T(8,128)(2,1)S(1)}, bf16[2,128,768]{2,1,0:T(8,128)(2,1)S(1)}, u32[]{:S(2)}, u32[]{:S(2)}) collective-permute-start(bf16[2,128,768]{2,1,0:T(8,128)(2,1)S(1)} %get-tuple-element.46), channel_id=1, source_target_pairs={{0,4},{1,5},{2,6},{3,7},{4,0},{5,1},{6,2},{7,3},{8,12},{9,13},{10,... | collective-permute-start | bytes 1179656 | tf_op jit(solution)/shard_map/ppermute | solution.py:271
  30.6 20.4 %collective-permute-start.4 = (bf16[2,128,768]{2,1,0:T(8,128)(2,1)S(1)}, bf16[2,128,768]{2,1,0:T(8,128)(2,1)S(1)}, u32[]{:S(2)}, u32[]{:S(2)}) collective-permute-start(bf16[2,128,768]{2,1,0:T(8,128)(2,1)S(1)} %get-tuple-element.48), channel_id=1, source_target_pairs={{0,2},{1,3},{2,0},{3,1},{4,6},{5,7},{6,4},{7,5},{8,10},{9,11},{10,... | collective-permute-start | bytes 1179656 | tf_op jit(solution)/shard_map/ppermute | solution.py:271
  45.3 12.3 %collective-permute-start.11 = (bf16[2,192,768]{2,1,0:T(8,128)(2,1)S(1)}, bf16[2,192,768]{2,1,0:T(8,128)(2,1)S(1)}, u32[]{:S(2)}, u32[]{:S(2)}) collective-permute-start(bf16[2,192,768]{2,1,0:T(8,128)(2,1)S(1)} %get-tuple-element.61), channel_id=1, source_target_pairs={{0,1},{1,0},{2,3},{3,2},{4,5},{5,4},{6,7},{7,6},{8,9},{9,8},{10,11... | collective-permute-start | bytes 1769480 | tf_op jit(solution)/shard_map/ppermute | solution.py:271
  45.3 21.3 %collective-permute-start.13 = (bf16[2,128,768]{2,1,0:T(8,128)(2,1)S(1)}, bf16[2,128,768]{2,1,0:T(8,128)(2,1)S(1)}, u32[]{:S(2)}, u32[]{:S(2)}) collective-permute-start(bf16[2,128,768]{2,1,0:T(8,128)(2,1)S(1)} %get-tuple-element.64), channel_id=1, source_target_pairs={{0,8},{1,9},{2,10},{3,11},{4,12},{5,13},{6,14},{7,15},{8,0},{9,1},... | collective-permute-start | bytes 1179656 | tf_op jit(solution)/shard_map/ppermute | solution.py:271
  48.7 19.5 %collective-permute-start.14 = (bf16[2,128,768]{2,1,0:T(8,128)(2,1)S(1)}, bf16[2,128,768]{2,1,0:T(8,128)(2,1)S(1)}, u32[]{:S(2)}, u32[]{:S(2)}) collective-permute-start(bf16[2,128,768]{2,1,0:T(8,128)(2,1)S(1)} %get-tuple-element.65), channel_id=1, source_target_pairs={{0,4},{1,5},{2,6},{3,7},{4,0},{5,1},{6,2},{7,3},{8,12},{9,13},{10,... | collective-permute-start | bytes 1179656 | tf_op jit(solution)/shard_map/ppermute | solution.py:271
  51.0 17.6 %collective-permute-start.15 = (bf16[2,128,768]{2,1,0:T(8,128)(2,1)S(1)}, bf16[2,128,768]{2,1,0:T(8,128)(2,1)S(1)}, u32[]{:S(2)}, u32[]{:S(2)}) collective-permute-start(bf16[2,128,768]{2,1,0:T(8,128)(2,1)S(1)} %get-tuple-element.66), channel_id=1, source_target_pairs={{0,2},{1,3},{2,0},{3,1},{4,6},{5,7},{6,4},{7,5},{8,10},{9,11},{10,... | collective-permute-start | bytes 1179656 | tf_op jit(solution)/shard_map/ppermute | solution.py:271
  57.5 29.7 %collective-permute-start.12 = (bf16[2,192,768]{2,1,0:T(8,128)(2,1)S(1)}, bf16[2,192,768]{2,1,0:T(8,128)(2,1)S(1)}, u32[]{:S(2)}, u32[]{:S(2)}) collective-permute-start(bf16[2,192,768]{2,1,0:T(8,128)(2,1)S(1)} %get-tuple-element.62), channel_id=1, source_target_pairs={{0,1},{1,0},{2,3},{3,2},{4,5},{5,4},{6,7},{7,6},{8,9},{9,8},{10,11... | collective-permute-start | bytes 1769480 | tf_op jit(solution)/shard_map/ppermute | solution.py:271
  57.6 13.5 %collective-permute-start.17 = (bf16[2,64,768]{2,1,0:T(8,128)(2,1)S(1)}, bf16[2,64,768]{2,1,0:T(8,128)(2,1)S(1)}, u32[]{:S(2)}, u32[]{:S(2)}) collective-permute-start(bf16[2,64,768]{2,1,0:T(8,128)(2,1)S(1)} %get-tuple-element.69), channel_id=1, source_target_pairs={{0,0},{1,2},{2,1},{3,4},{4,3},{5,6},{6,5},{7,8},{8,7},{9,10},{10,9... | collective-permute-start | bytes 589832 | tf_op jit(solution)/shard_map/ppermute | solution.py:271
  66.6 19.3 %collective-permute-start.8 = (bf16[2,128,768]{2,1,0:T(8,128)(2,1)S(1)}, bf16[2,128,768]{2,1,0:T(8,128)(2,1)S(1)}, u32[]{:S(2)}, u32[]{:S(2)}) collective-permute-start(bf16[2,128,768]{2,1,0:T(8,128)(2,1)S(1)} %get-tuple-element.57), channel_id=1, source_target_pairs={{0,8},{1,9},{2,10},{3,11},{4,12},{5,13},{6,14},{7,15},{8,0},{9,1},... | collective-permute-start | bytes 1179656 | tf_op jit(solution)/shard_map/ppermute | solution.py:271
  68.2 19.0 %collective-permute-start.9 = (bf16[2,128,768]{2,1,0:T(8,128)(2,1)S(1)}, bf16[2,128,768]{2,1,0:T(8,128)(2,1)S(1)}, u32[]{:S(2)}, u32[]{:S(2)}) collective-permute-start(bf16[2,128,768]{2,1,0:T(8,128)(2,1)S(1)} %get-tuple-element.58), channel_id=1, source_target_pairs={{0,4},{1,5},{2,6},{3,7},{4,0},{5,1},{6,2},{7,3},{8,12},{9,13},{10,... | collective-permute-start | bytes 1179656 | tf_op jit(solution)/shard_map/ppermute | solution.py:271
  68.7 18.5 %collective-permute-start.10 = (bf16[2,128,768]{2,1,0:T(8,128)(2,1)S(1)}, bf16[2,128,768]{2,1,0:T(8,128)(2,1)S(1)}, u32[]{:S(2)}, u32[]{:S(2)}) collective-permute-start(bf16[2,128,768]{2,1,0:T(8,128)(2,1)S(1)} %get-tuple-element.59), channel_id=1, source_target_pairs={{0,2},{1,3},{2,0},{3,1},{4,6},{5,7},{6,4},{7,5},{8,10},{9,11},{10,... | collective-permute-start | bytes 1179656 | tf_op jit(solution)/shard_map/ppermute | solution.py:271
  71.1 4.3 %collective-permute-start.16 = (bf16[2,64,768]{2,1,0:T(8,128)(2,1)S(1)}, bf16[2,64,768]{2,1,0:T(8,128)(2,1)S(1)}, u32[]{:S(2)}, u32[]{:S(2)}) collective-permute-start(bf16[2,64,768]{2,1,0:T(8,128)(2,1)S(1)} %get-tuple-element.67), channel_id=1, source_target_pairs={{0,0},{1,2},{2,1},{3,4},{4,3},{5,6},{6,5},{7,8},{8,7},{9,10},{10,9... | collective-permute-start | bytes 589832 | tf_op jit(solution)/shard_map/ppermute | solution.py:271

commit v3 on v1

--- a/solution.py
+++ b/solution.py
@@ -288,7 +288,7 @@
         *pieces, = pack(block_pick, *after((key_rows, value_rows), last), cut)
         last = pieces[:1]
         before = fetched[-1]
-        gates = [[before[0], *near] for i in range(far)]
+        gates = [[before[0], *near]] * (far - 1) + [[before[far - 1], *near]]
         pieces = [after([p], gate)[0] for p, gate in zip(pieces, gates, strict=True)]
         fetched.append(send(pieces, pairs[:far]))
     fetched = [got + near + edge for got in fetched]

time: 90.4 us -> 90.5 us (level)
  transfers between devices with their start and end apart: 18 -> 18, of which waited for: 7 -> 8; matrix products, arithmetic and copies ran while one was open for 2% -> 2% of each run, Pallas kernels for 19% -> 19%
where the time goes in v3:
time: 90.5 us; the launch traced here: 89.3 us
  waiting for transfers between devices  42.1 us (47%)
  starting transfers between devices  22.7 us (25%)
  Pallas kernels  21.1 us (23%)
  local copies, waits for them, and re-layouts  2.55 us (3%)
    ppermute x18, waiting for transfers between devices, send(): lax.ppermute(piece, 'frame', t)  42.1 us
    ppermute x18, starting transfers between devices, send(): lax.ppermute(piece, 'frame', t)  22.7 us
    pallas_call x2, Pallas kernels, attend(): pl.pallas_call(functools.partial(attend_kernel, head, heads, rows, len(al...  13 us
    pallas_call x2, Pallas kernels, pack(): pl.pallas_call(functools.partial(pack_kernel, pieces), out_shape=[pltpu.V...  4.38 us
    pallas_call x2, Pallas kernels, combine(): pl.pallas_call(functools.partial(combine_kernel, head, heads, rows, len(a...  3.74 us
    unnamed x16, local copies, waits for them, and re-layouts  2.55 us
  transfers between devices with their start and end apart: 18, of which 8 were waited for; matrix products, arithmetic and copies ran while one was open for 2% of the time, Pallas kernels for 19%

profile of v3, /device:TPU:0, one launch (start us, length us, event | category | flops | bytes accessed | tf_op | source)
XLA Modules:
  0.0 89.3 jit_solution(5606984094489264491)
XLA Ops:
  0.7 0.8 copy-done.2
  1.4 2.4 %shard_map.93 = (bf16[2,192,1536]{2,1,0:T(8,128)(2,1)S(1)}, bf16[2,64,1536]{2,1,0:T(8,128)(2,1)S(1)}, bf16[2,128,768]{2,1,0:T(8,128)(2,1)S(1)}, bf16[2,128,768]{2,1,0:T(8,128)(2,1)S(1)}, bf16[2,128,768]{2,1,0:T(8,128)(2,1)S(1)}) custom-call(s32[1,4]{1,0:T(1,128)S(1)} %copy-done.2, bf16[256,1536]{1,0:T(8,128)(2,1)} %refs_2_.3, bf16[256,1536]{1,0:T(8,128)(2,1)} %refs_3_.3), custom_call_target="tpu_custom_call" | custom-call | bytes 5505024 | tf_op jit(solution)/shard_map/pallas_call | solution.py:76
  3.9 0.5 collective-permute-start.1
  4.4 2.6 %collective-permute-start.4 = (bf16[2,128,768]{2,1,0:T(8,128)(2,1)S(1)}, bf16[2,128,768]{2,1,0:T(8,128)(2,1)S(1)}, u32[]{:S(2)}, u32[]{:S(2)}) collective-permute-start(bf16[2,128,768]{2,1,0:T(8,128)(2,1)S(1)} %get-tuple-element.48), channel_id=1, source_target_pairs={{0,2},{1,3},{2,0},{3,1},{4,6},{5,7},{6,4},{7,5},{8,10},{9,11},{10,... | collective-permute-start | bytes 1179656 | tf_op jit(solution)/shard_map/ppermute | solution.py:266
  7.0 2.8 %collective-permute-start = (bf16[2,128,768]{2,1,0:T(8,128)(2,1)S(1)}, bf16[2,128,768]{2,1,0:T(8,128)(2,1)S(1)}, u32[]{:S(2)}, u32[]{:S(2)}) collective-permute-start(bf16[2,128,768]{2,1,0:T(8,128)(2,1)S(1)} %get-tuple-element.39), channel_id=1, source_target_pairs={{0,8},{1,9},{2,10},{3,11},{4,12},{5,13},{6,14},{7,15},{8,0},{9,1},... | collective-permute-start | bytes 1179656 | tf_op jit(solution)/shard_map/ppermute | solution.py:266
  9.8 0.7 collective-permute-start.6
  10.4 2.8 %collective-permute-start.7 = (bf16[2,128,768]{2,1,0:T(8,128)(2,1)S(1)}, bf16[2,128,768]{2,1,0:T(8,128)(2,1)S(1)}, u32[]{:S(2)}, u32[]{:S(2)}) collective-permute-start(bf16[2,128,768]{2,1,0:T(8,128)(2,1)S(1)} %get-tuple-element.51), channel_id=1, source_target_pairs={{0,4},{1,5},{2,6},{3,7},{4,0},{5,1},{6,2},{7,3},{8,12},{9,13},{10,... | collective-permute-start | bytes 1179656 | tf_op jit(solution)/shard_map/ppermute | solution.py:266
  13.3 1.9 %shard_map.94 = (bf16[2,128,768]{2,1,0:T(8,128)(2,1)S(1)}, bf16[2,128,768]{2,1,0:T(8,128)(2,1)S(1)}, bf16[2,128,768]{2,1,0:T(8,128)(2,1)S(1)}) custom-call(s32[1,4]{1,0:T(1,128)S(1)} %copy-done.3, bf16[256,1536]{1,0:T(8,128)(2,1)} %refs_2_.3, bf16[256,1536]{1,0:T(8,128)(2,1)} %refs_3_.3), custom_call_target="tpu_custom_call" | custom-call | bytes 2359296 | tf_op jit(solution)/shard_map/pallas_call | solution.py:76
  15.2 3.6 %collective-permute-done.4.refs_6_ = bf16[2,128,768]{2,1,0:T(8,128)(2,1)S(1)} collective-permute-done((bf16[2,128,768]{2,1,0:T(8,128)(2,1)S(1)}, bf16[2,128,768]{2,1,0:T(8,128)(2,1)S(1)}, u32[]{:S(2)}, u32[]{:S(2)}) %collective-permute-start.4) | collective-permute-done | bytes 393248 | tf_op jit(solution)/shard_map/ppermute | solution.py:266
  18.8 9.0 %collective-permute-done.refs_4_ = bf16[2,128,768]{2,1,0:T(8,128)(2,1)S(1)} collective-permute-done((bf16[2,128,768]{2,1,0:T(8,128)(2,1)S(1)}, bf16[2,128,768]{2,1,0:T(8,128)(2,1)S(1)}, u32[]{:S(2)}, u32[]{:S(2)}) %collective-permute-start) | collective-permute-done | bytes 393248 | tf_op jit(solution)/shard_map/ppermute | solution.py:266
  27.7 4.1 %collective-permute-start.3 = (bf16[2,128,768]{2,1,0:T(8,128)(2,1)S(1)}, bf16[2,128,768]{2,1,0:T(8,128)(2,1)S(1)}, u32[]{:S(2)}, u32[]{:S(2)}) collective-permute-start(bf16[2,128,768]{2,1,0:T(8,128)(2,1)S(1)} %get-tuple-element.46), channel_id=1, source_target_pairs={{0,4},{1,5},{2,6},{3,7},{4,0},{5,1},{6,2},{7,3},{8,12},{9,13},{10,... | collective-permute-start | bytes 1179656 | tf_op jit(solution)/shard_map/ppermute | solution.py:266
  31.8 0.4 collective-permute-start.5
  32.3 6.5 %collective-permute-done.7.refs_5_ = bf16[2,128,768]{2,1,0:T(8,128)(2,1)S(1)} collective-permute-done((bf16[2,128,768]{2,1,0:T(8,128)(2,1)S(1)}, bf16[2,128,768]{2,1,0:T(8,128)(2,1)S(1)}, u32[]{:S(2)}, u32[]{:S(2)}) %collective-permute-start.7) | collective-permute-done | bytes 393248 | tf_op jit(solution)/shard_map/ppermute | solution.py:266
  38.8 6.5 %shard_map.95 = (bf16[256,1536]{1,0:T(8,128)(2,1)S(1)}, bf16[256,1536]{1,0:T(8,128)(2,1)S(1)}, f32[2,256,768]{2,1,0:T(8,128)S(1)}, bf16[2,128,768]{2,1,0:T(8,128...) custom-call(s32[1,2,4]{2,1,0:T(2,128)S(1)} %bitcast.1, ...), custom_call_target="tpu_custom_call" | custom-call | flops 2113929216 | bytes 7864320 | tf_op jit(solution)/shard_map/pallas_call | solution.py:183
  45.3 0.1 collective-permute-start.11
  45.4 3.6 %collective-permute-start.13 = (bf16[2,128,768]{2,1,0:T(8,128)(2,1)S(1)}, bf16[2,128,768]{2,1,0:T(8,128)(2,1)S(1)}, u32[]{:S(2)}, u32[]{:S(2)}) collective-permute-start(bf16[2,128,768]{2,1,0:T(8,128)(2,1)S(1)} %get-tuple-element.64), channel_id=1, source_target_pairs={{0,8},{1,9},{2,10},{3,11},{4,12},{5,13},{6,14},{7,15},{8,0},{9,1},... | collective-permute-start | bytes 1179656 | tf_op jit(solution)/shard_map/ppermute | solution.py:266
  49.0 2.7 %collective-permute-done.3.refs_5_ = bf16[2,128,768]{2,1,0:T(8,128)(2,1)S(1)} collective-permute-done((bf16[2,128,768]{2,1,0:T(8,128)(2,1)S(1)}, bf16[2,128,768]{2,1,0:T(8,128)(2,1)S(1)}, u32[]{:S(2)}, u32[]{:S(2)}) %collective-permute-start.3) | collective-permute-done | bytes 393248 | tf_op jit(solution)/shard_map/ppermute | solution.py:266
  51.7 1.9 %collective-permute-start.15 = (bf16[2,128,768]{2,1,0:T(8,128)(2,1)S(1)}, bf16[2,128,768]{2,1,0:T(8,128)(2,1)S(1)}, u32[]{:S(2)}, u32[]{:S(2)}) collective-permute-start(bf16[2,128,768]{2,1,0:T(8,128)(2,1)S(1)} %get-tuple-element.66), channel_id=1, source_target_pairs={{0,2},{1,3},{2,0},{3,1},{4,6},{5,7},{6,4},{7,5},{8,10},{9,11},{10,... | collective-permute-start | bytes 1179656 | tf_op jit(solution)/shard_map/ppermute | solution.py:266
  53.6 6.5 %shard_map.96 = (bf16[256,1536]{1,0:T(8,128)(2,1)S(1)}, bf16[256,1536]{1,0:T(8,128)(2,1)S(1)}, f32[2,256,768]{2,1,0:T(8,128)S(1)}, bf16[2,128,768]{2,1,0:T(8,128...) custom-call(s32[1,2,4]{2,1,0:T(2,128)S(1)} %bitcast.2, ...), custom_call_target="tpu_custom_call", output_to_operand_aliasing={{0}: (10, {}), {1}: (11, {})} | custom-call | flops 2113929216 | bytes 7864320 | tf_op jit(solution)/shard_map/pallas_call | solution.py:183
  60.1 0.1 collective-permute-start.12
  60.2 0.7 collective-permute-start.17
  60.9 5.8 %collective-permute-done.13.refs_0_ = bf16[2,128,768]{2,1,0:T(8,128)(2,1)S(1)} collective-permute-done((bf16[2,128,768]{2,1,0:T(8,128)(2,1)S(1)}, bf16[2,128,768]{2,1,0:T(8,128)(2,1)S(1)}, u32[]{:S(2)}, u32[]{:S(2)}) %collective-permute-start.13) | collective-permute-done | bytes 393248 | tf_op jit(solution)/shard_map/ppermute | solution.py:266
  66.7 1.8 %collective-permute-done.14.refs_1_ = bf16[2,128,768]{2,1,0:T(8,128)(2,1)S(1)} collective-permute-done((bf16[2,128,768]{2,1,0:T(8,128)(2,1)S(1)}, bf16[2,128,768]{2,1,0:T(8,128)(2,1)S(1)}, u32[]{:S(2)}, u32[]{:S(2)}) %collective-permute-start.14) | collective-permute-done | bytes 393248 | tf_op jit(solution)/shard_map/ppermute | solution.py:266
  68.4 0.5 collective-permute-start.9
  69.0 1.3 %collective-permute-start.10 = (bf16[2,128,768]{2,1,0:T(8,128)(2,1)S(1)}, bf16[2,128,768]{2,1,0:T(8,128)(2,1)S(1)}, u32[]{:S(2)}, u32[]{:S(2)}) collective-permute-start(bf16[2,128,768]{2,1,0:T(8,128)(2,1)S(1)} %get-tuple-element.59), channel_id=1, source_target_pairs={{0,2},{1,3},{2,0},{3,1},{4,6},{5,7},{6,4},{7,5},{8,10},{9,11},{10,... | collective-permute-start | bytes 1179656 | tf_op jit(solution)/shard_map/ppermute | solution.py:266
  70.2 0.7 collective-permute-start.16
  70.9 0.9 copy.18
  71.8 0.9 copy.19
  72.7 1.9 %shard_map.97 = (bf16[256,1536]{1,0:T(8,128)(2,1)}, bf16[256,1536]{1,0:T(8,128)(2,1)}) custom-call(s32[1,4]{1,0:T(1,128)S(1)} %copy-done.3, f32[2,256,768]{2,1,0:T(8,128)S(1)} %get-tuple-element.68.own_ref, bf16[2,128,768]{2,1,0:T(8,128)(2,1)S(1)} %collective-permute-done.13.refs_0_, bf16[2,128,768]{2,1,0:T(8,128)(2,1)S(1)} %collective-permute-done.14.refs_1_, ...), custom_call_target="tpu_custom_call" | custom-call | bytes 3145728 | tf_op jit(solution)/shard_map/pallas_call | solution.py:234
  74.6 11.6 %collective-permute-done.8.refs_0_ = bf16[2,128,768]{2,1,0:T(8,128)(2,1)S(1)} collective-permute-done((bf16[2,128,768]{2,1,0:T(8,128)(2,1)S(1)}, bf16[2,128,768]{2,1,0:T(8,128)(2,1)S(1)}, u32[]{:S(2)}, u32[]{:S(2)}) %collective-permute-start.8) | collective-permute-done | bytes 393248 | tf_op jit(solution)/shard_map/ppermute | solution.py:266
  86.2 1.2 %collective-permute-done.9.refs_1_ = bf16[2,128,768]{2,1,0:T(8,128)(2,1)S(1)} collective-permute-done((bf16[2,128,768]{2,1,0:T(8,128)(2,1)S(1)}, bf16[2,128,768]{2,1,0:T(8,128)(2,1)S(1)}, u32[]{:S(2)}, u32[]{:S(2)}) %collective-permute-start.9) | collective-permute-done | bytes 393248 | tf_op jit(solution)/shard_map/ppermute | solution.py:266
  87.4 1.9 %shard_map.98 = (bf16[256,1536]{1,0:T(8,128)(2,1)}, bf16[256,1536]{1,0:T(8,128)(2,1)}) custom-call(s32[1,4]{1,0:T(1,128)S(1)} %copy-done.3, f32[2,256,768]{2,1,0:T(8,128)S(1)} %get-tuple-element.56.own_ref, bf16[2,128,768]{2,1,0:T(8,128)(2,1)S(1)} %collective-permute-done.8.refs_0_, ...), custom_call_target="tpu_custom_call", output_to_operand_aliasing={{0}: (7, {}), {1}: (8, {})} | custom-call | bytes 3145728 | tf_op jit(solution)/shard_map/pallas_call | solution.py:234
  (26 shorter events, 0.1 us)
Async XLA Ops:
  0.6 38.2 %copy-start.1 = (bf16[256,1536]{1,0:T(8,128)(2,1)S(1)}, bf16[256,1536]{1,0:T(8,128)(2,1)}, u32[]{:S(2)}) copy-start(bf16[256,1536]{1,0:T(8,128)(2,1)} %refs_3_.3) | copy-start | bytes 2359300
  0.6 38.2 %copy-start = (bf16[256,1536]{1,0:T(8,128)(2,1)S(1)}, bf16[256,1536]{1,0:T(8,128)(2,1)}, u32[]{:S(2)}) copy-start(bf16[256,1536]{1,0:T(8,128)(2,1)} %refs_2_.3) | copy-start | bytes 2359300
  0.7 0.8 copy-start.2
  1.4 11.8 %copy-start.3 = (s32[1,4]{1,0:T(1,128)S(1)}, s32[1,4]{1,0:T(1,128)}, u32[]{:S(2)}) copy-start(s32[1,4]{1,0:T(1,128)} %pick_ref.7) | copy-start | bytes 52
  1.4 37.4 %copy-start.4 = (bf16[256,1536]{1,0:T(8,128)(2,1)S(1)}, bf16[256,1536]{1,0:T(8,128)(2,1)}, u32[]{:S(2)}) copy-start(bf16[256,1536]{1,0:T(8,128)(2,1)} %refs_0_.3) | copy-start | bytes 2359300
  1.4 37.4 %copy-start.5 = (bf16[256,1536]{1,0:T(8,128)(2,1)S(1)}, bf16[256,1536]{1,0:T(8,128)(2,1)}, u32[]{:S(2)}) copy-start(bf16[256,1536]{1,0:T(8,128)(2,1)} %refs_1_.3) | copy-start | bytes 2359300
  1.4 37.4 %copy-start.6 = (s32[1,4,2]{1,2,0:T(2,128)S(1)}, s32[1,4,2]{1,2,0:T(2,128)}, u32[]{:S(2)}) copy-start(s32[1,4,2]{1,2,0:T(2,128)} %param.10) | copy-start | bytes 100
  3.9 14.9 %collective-permute-start.1 = (bf16[2,192,1536]{2,1,0:T(8,128)(2,1)S(1)}, bf16[2,192,1536]{2,1,0:T(8,128)(2,1)S(1)}, u32[]{:S(2)}, u32[]{:S(2)}) collective-permute-start(bf16[2,192,1536]{2,1,0:T(8,128)(2,1)S(1)} %get-tuple-element.43), channel_id=1, source_target_pairs={{0,1},{1,0},{2,3},{3,2},{4,5},{5,4},{6,7},{7,6},{8,9},{9,8},{10,11... | collective-permute-start | bytes 3538952 | tf_op jit(solution)/shard_map/ppermute | solution.py:266
  4.4 14.4 %collective-permute-start.4 = (bf16[2,128,768]{2,1,0:T(8,128)(2,1)S(1)}, bf16[2,128,768]{2,1,0:T(8,128)(2,1)S(1)}, u32[]{:S(2)}, u32[]{:S(2)}) collective-permute-start(bf16[2,128,768]{2,1,0:T(8,128)(2,1)S(1)} %get-tuple-element.48), channel_id=1, source_target_pairs={{0,2},{1,3},{2,0},{3,1},{4,6},{5,7},{6,4},{7,5},{8,10},{9,11},{10,... | collective-permute-start | bytes 1179656 | tf_op jit(solution)/shard_map/ppermute | solution.py:266
  7.0 20.8 %collective-permute-start = (bf16[2,128,768]{2,1,0:T(8,128)(2,1)S(1)}, bf16[2,128,768]{2,1,0:T(8,128)(2,1)S(1)}, u32[]{:S(2)}, u32[]{:S(2)}) collective-permute-start(bf16[2,128,768]{2,1,0:T(8,128)(2,1)S(1)} %get-tuple-element.39), channel_id=1, source_target_pairs={{0,8},{1,9},{2,10},{3,11},{4,12},{5,13},{6,14},{7,15},{8,0},{9,1},... | collective-permute-start | bytes 1179656 | tf_op jit(solution)/shard_map/ppermute | solution.py:266
  9.8 22.5 %collective-permute-start.6 = (bf16[2,64,1536]{2,1,0:T(8,128)(2,1)S(1)}, bf16[2,64,1536]{2,1,0:T(8,128)(2,1)S(1)}, u32[]{:S(2)}, u32[]{:S(2)}) collective-permute-start(bf16[2,64,1536]{2,1,0:T(8,128)(2,1)S(1)} %get-tuple-element.50), channel_id=1, source_target_pairs={{0,0},{1,2},{2,1},{3,4},{4,3},{5,6},{6,5},{7,8},{8,7},{9,10},{10,9... | collective-permute-start | bytes 1179656 | tf_op jit(solution)/shard_map/ppermute | solution.py:266
  10.4 28.3 %collective-permute-start.7 = (bf16[2,128,768]{2,1,0:T(8,128)(2,1)S(1)}, bf16[2,128,768]{2,1,0:T(8,128)(2,1)S(1)}, u32[]{:S(2)}, u32[]{:S(2)}) collective-permute-start(bf16[2,128,768]{2,1,0:T(8,128)(2,1)S(1)} %get-tuple-element.51), channel_id=1, source_target_pairs={{0,4},{1,5},{2,6},{3,7},{4,0},{5,1},{6,2},{7,3},{8,12},{9,13},{10,... | collective-permute-start | bytes 1179656 | tf_op jit(solution)/shard_map/ppermute | solution.py:266
  27.7 21.3 %collective-permute-start.2 = (bf16[2,128,768]{2,1,0:T(8,128)(2,1)S(1)}, bf16[2,128,768]{2,1,0:T(8,128)(2,1)S(1)}, u32[]{:S(2)}, u32[]{:S(2)}) collective-permute-start(bf16[2,128,768]{2,1,0:T(8,128)(2,1)S(1)} %get-tuple-element.44), channel_id=1, source_target_pairs={{0,8},{1,9},{2,10},{3,11},{4,12},{5,13},{6,14},{7,15},{8,0},{9,1},... | collective-permute-start | bytes 1179656 | tf_op jit(solution)/shard_map/ppermute | solution.py:266
  27.7 24.0 %collective-permute-start.3 = (bf16[2,128,768]{2,1,0:T(8,128)(2,1)S(1)}, bf16[2,128,768]{2,1,0:T(8,128)(2,1)S(1)}, u32[]{:S(2)}, u32[]{:S(2)}) collective-permute-start(bf16[2,128,768]{2,1,0:T(8,128)(2,1)S(1)} %get-tuple-element.46), channel_id=1, source_target_pairs={{0,4},{1,5},{2,6},{3,7},{4,0},{5,1},{6,2},{7,3},{8,12},{9,13},{10,... | collective-permute-start | bytes 1179656 | tf_op jit(solution)/shard_map/ppermute | solution.py:266
  31.8 21.8 %collective-permute-start.5 = (bf16[2,128,768]{2,1,0:T(8,128)(2,1)S(1)}, bf16[2,128,768]{2,1,0:T(8,128)(2,1)S(1)}, u32[]{:S(2)}, u32[]{:S(2)}) collective-permute-start(bf16[2,128,768]{2,1,0:T(8,128)(2,1)S(1)} %get-tuple-element.49), channel_id=1, source_target_pairs={{0,2},{1,3},{2,0},{3,1},{4,6},{5,7},{6,4},{7,5},{8,10},{9,11},{10,... | collective-permute-start | bytes 1179656 | tf_op jit(solution)/shard_map/ppermute | solution.py:266
  45.3 14.8 %collective-permute-start.11 = (bf16[2,192,768]{2,1,0:T(8,128)(2,1)S(1)}, bf16[2,192,768]{2,1,0:T(8,128)(2,1)S(1)}, u32[]{:S(2)}, u32[]{:S(2)}) collective-permute-start(bf16[2,192,768]{2,1,0:T(8,128)(2,1)S(1)} %get-tuple-element.61), channel_id=1, source_target_pairs={{0,1},{1,0},{2,3},{3,2},{4,5},{5,4},{6,7},{7,6},{8,9},{9,8},{10,11... | collective-permute-start | bytes 1769480 | tf_op jit(solution)/shard_map/ppermute | solution.py:266
  45.4 21.2 %collective-permute-start.13 = (bf16[2,128,768]{2,1,0:T(8,128)(2,1)S(1)}, bf16[2,128,768]{2,1,0:T(8,128)(2,1)S(1)}, u32[]{:S(2)}, u32[]{:S(2)}) collective-permute-start(bf16[2,128,768]{2,1,0:T(8,128)(2,1)S(1)} %get-tuple-element.64), channel_id=1, source_target_pairs={{0,8},{1,9},{2,10},{3,11},{4,12},{5,13},{6,14},{7,15},{8,0},{9,1},... | collective-permute-start | bytes 1179656 | tf_op jit(solution)/shard_map/ppermute | solution.py:266
  49.0 19.4 %collective-permute-start.14 = (bf16[2,128,768]{2,1,0:T(8,128)(2,1)S(1)}, bf16[2,128,768]{2,1,0:T(8,128)(2,1)S(1)}, u32[]{:S(2)}, u32[]{:S(2)}) collective-permute-start(bf16[2,128,768]{2,1,0:T(8,128)(2,1)S(1)} %get-tuple-element.65), channel_id=1, source_target_pairs={{0,4},{1,5},{2,6},{3,7},{4,0},{5,1},{6,2},{7,3},{8,12},{9,13},{10,... | collective-permute-start | bytes 1179656 | tf_op jit(solution)/shard_map/ppermute | solution.py:266
  51.7 17.2 %collective-permute-start.15 = (bf16[2,128,768]{2,1,0:T(8,128)(2,1)S(1)}, bf16[2,128,768]{2,1,0:T(8,128)(2,1)S(1)}, u32[]{:S(2)}, u32[]{:S(2)}) collective-permute-start(bf16[2,128,768]{2,1,0:T(8,128)(2,1)S(1)} %get-tuple-element.66), channel_id=1, source_target_pairs={{0,2},{1,3},{2,0},{3,1},{4,6},{5,7},{6,4},{7,5},{8,10},{9,11},{10,... | collective-permute-start | bytes 1179656 | tf_op jit(solution)/shard_map/ppermute | solution.py:266
  60.1 27.3 %collective-permute-start.12 = (bf16[2,192,768]{2,1,0:T(8,128)(2,1)S(1)}, bf16[2,192,768]{2,1,0:T(8,128)(2,1)S(1)}, u32[]{:S(2)}, u32[]{:S(2)}) collective-permute-start(bf16[2,192,768]{2,1,0:T(8,128)(2,1)S(1)} %get-tuple-element.62), channel_id=1, source_target_pairs={{0,1},{1,0},{2,3},{3,2},{4,5},{5,4},{6,7},{7,6},{8,9},{9,8},{10,11... | collective-permute-start | bytes 1769480 | tf_op jit(solution)/shard_map/ppermute | solution.py:266
  60.2 10.0 %collective-permute-start.17 = (bf16[2,64,768]{2,1,0:T(8,128)(2,1)S(1)}, bf16[2,64,768]{2,1,0:T(8,128)(2,1)S(1)}, u32[]{:S(2)}, u32[]{:S(2)}) collective-permute-start(bf16[2,64,768]{2,1,0:T(8,128)(2,1)S(1)} %get-tuple-element.69), channel_id=1, source_target_pairs={{0,0},{1,2},{2,1},{3,4},{4,3},{5,6},{6,5},{7,8},{8,7},{9,10},{10,9... | collective-permute-start | bytes 589832 | tf_op jit(solution)/shard_map/ppermute | solution.py:266
  66.7 19.5 %collective-permute-start.8 = (bf16[2,128,768]{2,1,0:T(8,128)(2,1)S(1)}, bf16[2,128,768]{2,1,0:T(8,128)(2,1)S(1)}, u32[]{:S(2)}, u32[]{:S(2)}) collective-permute-start(bf16[2,128,768]{2,1,0:T(8,128)(2,1)S(1)} %get-tuple-element.57), channel_id=1, source_target_pairs={{0,8},{1,9},{2,10},{3,11},{4,12},{5,13},{6,14},{7,15},{8,0},{9,1},... | collective-permute-start | bytes 1179656 | tf_op jit(solution)/shard_map/ppermute | solution.py:266
  68.4 19.0 %collective-permute-start.9 = (bf16[2,128,768]{2,1,0:T(8,128)(2,1)S(1)}, bf16[2,128,768]{2,1,0:T(8,128)(2,1)S(1)}, u32[]{:S(2)}, u32[]{:S(2)}) collective-permute-start(bf16[2,128,768]{2,1,0:T(8,128)(2,1)S(1)} %get-tuple-element.58), channel_id=1, source_target_pairs={{0,4},{1,5},{2,6},{3,7},{4,0},{5,1},{6,2},{7,3},{8,12},{9,13},{10,... | collective-permute-start | bytes 1179656 | tf_op jit(solution)/shard_map/ppermute | solution.py:266
  69.0 18.4 %collective-permute-start.10 = (bf16[2,128,768]{2,1,0:T(8,128)(2,1)S(1)}, bf16[2,128,768]{2,1,0:T(8,128)(2,1)S(1)}, u32[]{:S(2)}, u32[]{:S(2)}) collective-permute-start(bf16[2,128,768]{2,1,0:T(8,128)(2,1)S(1)} %get-tuple-element.59), channel_id=1, source_target_pairs={{0,2},{1,3},{2,0},{3,1},{4,6},{5,7},{6,4},{7,5},{8,10},{9,11},{10,... | collective-permute-start | bytes 1179656 | tf_op jit(solution)/shard_map/ppermute | solution.py:266
  70.2 4.3 %collective-permute-start.16 = (bf16[2,64,768]{2,1,0:T(8,128)(2,1)S(1)}, bf16[2,64,768]{2,1,0:T(8,128)(2,1)S(1)}, u32[]{:S(2)}, u32[]{:S(2)}) collective-permute-start(bf16[2,64,768]{2,1,0:T(8,128)(2,1)S(1)} %get-tuple-element.67), channel_id=1, source_target_pairs={{0,0},{1,2},{2,1},{3,4},{4,3},{5,6},{6,5},{7,8},{8,7},{9,10},{10,9... | collective-permute-start | bytes 589832 | tf_op jit(solution)/shard_map/ppermute | solution.py:266
